TPU v7x, 768 devices: a whole 4x8x12 slice. The times are simulated.
768 devices in a mesh: region: 12 (over z), head: 64 (over x, y, core).
Axes of the slice: x: 4, y: 8, z: 12, core: 2. Of those that a mesh axis runs over, the one named last changes fastest.
Arguments:
- query: bfloat16 [98304, 2048], P(('region', 'head')), may hold values from -6 to 6
- output: bfloat16 [98304, 2048], P(('region', 'head')), may hold values from -6 to 6
- grad_out: bfloat16 [98304, 2048], P(('region', 'head')), may hold values from -6 to 6
- log_norm: float32 [32, 98304], P(None, 'region'), may hold values from 3 to 5
- global_kv: bfloat16 [1536, 4096], P('region'), may hold values from -6 to 6
- block_ids: int32 [1536, 8], P('region'), may hold values from 0 to 23, as said below
- block_counts: int32 [1536], P('region'), may hold values from 1 to 8, as said below
Outputs:
- query_grad: bfloat16 [98304, 2048], P(('region', 'head'))
- kv_grad: float32 [1536, 4096], P('region', 'head')
Inputs may be any that keep to these rules, and one draw needn't show every extreme that they name: `block_ids`: each row names 8 different global blocks; entries at or beyond the row's count are ignored. `block_counts`: number of leading entries of a boundary block's intersection list that are live.
All inputs are finite; a program needn't handle non-finite values.
Results may differ from a plain program's by a relative error of at most 0.007.
Values may be sent and summed in bfloat16 or wider, within the bound.
No kernel may reach another device: no remote copies, remote signals or barrier semaphores. Data moves between devices by JAX's collectives and lax.ppermute only.
A program may use at most 64 MiB of HBM per device.

v0:
```python
import math

import jax
import jax.numpy as jnp
from jax import lax
from jax.sharding import PartitionSpec as P

HEADS = 32
HD = 64
BLOCK = 64


def from_partner(block, axis, bit):
    count = lax.axis_size(axis)
    route = []
    for low in range(count):
        high = low | 1 << bit
        if high != low and high < count:
            route += [(low, high), (high, low)]
    return lax.ppermute(block, axis, route)


def heads_layout(values, group_count, col_width):
    row_count = values.shape[0]
    half_rows = row_count // 2
    shaped = values.reshape(2, half_rows, group_count, col_width).transpose(2, 0, 1, 3)
    return shaped.reshape(2 * group_count, half_rows, col_width)


def delta_layout(values, group_count, heads_local):
    row_count = values.shape[0]
    half_rows = row_count // 2
    shaped = values.reshape(2, half_rows, group_count, heads_local).transpose(2, 0, 3, 1)
    return shaped.reshape(2 * group_count, heads_local, half_rows)


def body(query, output, grad_out, log_norm, global_kv, block_ids, block_counts):
    head_count = lax.axis_size("head")
    group_count = head_count // 2
    heads_local = HEADS // group_count
    col_width = heads_local * HD
    pair_width = 2 * col_width
    member = lax.axis_index("head")
    my_group = member // 2
    my_share = member % 2
    row_count = query.shape[0]
    half_rows = row_count // 2
    score_scale = 1.0 / math.sqrt(HD)
    max_slots = block_ids.shape[1]
    block_total = head_count * half_rows // BLOCK
    token_delta = jnp.sum(
        grad_out.astype(jnp.float32).reshape(row_count, HEADS, HD)
        * output.astype(jnp.float32).reshape(row_count, HEADS, HD),
        axis=-1,
    )
    query_recv, grad_recv = (
        lax.all_to_all(
            heads_layout(query, group_count, col_width),
            "head",
            split_axis=0,
            concat_axis=1,
            tiled=True,
        ),
        lax.all_to_all(
            heads_layout(grad_out, group_count, col_width),
            "head",
            split_axis=0,
            concat_axis=1,
            tiled=True,
        ),
    )
    delta_recv = lax.all_to_all(
        delta_layout(token_delta, group_count, heads_local),
        "head",
        split_axis=0,
        concat_axis=2,
        tiled=True,
    )
    grad_heads = grad_recv.reshape(block_total, BLOCK, heads_local, HD).transpose(2, 0, 1, 3)
    row_delta = delta_recv.reshape(heads_local, block_total, BLOCK)
    query_heads = query_recv.reshape(block_total, BLOCK, heads_local, HD).transpose(2, 0, 1, 3)
    norm_local = log_norm.reshape(group_count, heads_local, head_count, 2, half_rows)
    norm_local = lax.dynamic_index_in_dim(norm_local, my_group, axis=0, keepdims=False)
    norm_local = lax.dynamic_index_in_dim(norm_local, my_share, axis=2, keepdims=False)
    norm_rows = norm_local
    share_blocks = row_count // (2 * BLOCK)
    ids_mine = lax.dynamic_index_in_dim(
        block_ids.reshape(head_count, 2, share_blocks, max_slots), my_share, axis=1, keepdims=False
    )
    ids_mine = ids_mine.reshape(block_total, max_slots)
    counts_mine = lax.dynamic_index_in_dim(
        block_counts.reshape(head_count, 2, share_blocks), my_share, axis=1, keepdims=False
    )
    counts_mine = counts_mine.reshape(block_total)
    kv_mine = lax.dynamic_slice_in_dim(global_kv, my_group * pair_width, pair_width, 1)
    kv_whole = lax.all_gather(kv_mine, "region", axis=0, tiled=True)
    global_blocks = kv_whole.shape[0] // BLOCK
    kv_blocks = kv_whole.reshape(global_blocks, BLOCK, heads_local, 2 * HD).transpose(2, 0, 1, 3)
    turn_total = max_slots // 2

    def one_turn(turn_index, state):
        query_acc, kv_grads = state
        pair_ids = lax.dynamic_slice_in_dim(ids_mine, 2 * turn_index, 2, 1)
        slot_live = (2 * turn_index + jnp.arange(2, dtype=jnp.int32))[None, :] < counts_mine[
            :, None
        ]
        key_live = jnp.broadcast_to(slot_live[:, :, None], (block_total, 2, BLOCK)).reshape(
            block_total, 2 * BLOCK
        )
        fetched = kv_blocks[:, pair_ids].reshape(heads_local, block_total, 2 * BLOCK, 2 * HD)
        key_block = fetched[..., :HD]
        value_block = fetched[..., HD:]
        scores = (
            jnp.einsum(
                "hbtd,hbud->hbtu", query_heads, key_block, preferred_element_type=jnp.float32
            )
            * score_scale
        )
        weights = (
            jnp.exp(scores - norm_rows[..., None]) * key_live.astype(jnp.float32)[None, :, None, :]
        )
        weight_grad = jnp.einsum(
            "hbtd,hbud->hbtu", grad_heads, value_block, preferred_element_type=jnp.float32
        )
        score_grad = (weights * (weight_grad - row_delta[..., None])).astype(jnp.bfloat16)
        query_acc = query_acc + jnp.einsum(
            "hbtu,hbud->hbtd", score_grad, key_block, preferred_element_type=jnp.float32
        )
        key_grad = (
            jnp.einsum(
                "hbtu,hbtd->hbud", score_grad, query_heads, preferred_element_type=jnp.float32
            )
            * score_scale
        )
        value_grad = jnp.einsum(
            "hbtu,hbtd->hbud",
            weights.astype(jnp.bfloat16),
            grad_heads,
            preferred_element_type=jnp.float32,
        )
        pieces = jnp.concatenate([key_grad, value_grad], axis=-1).reshape(
            heads_local, block_total, 2, BLOCK, 2 * HD
        )
        kv_grads = kv_grads.at[:, pair_ids].add(pieces)
        return (query_acc, kv_grads)

    query_start = jnp.zeros((heads_local, block_total, BLOCK, HD), jnp.float32)
    grads_start = jnp.zeros((heads_local, global_blocks, BLOCK, 2 * HD), jnp.float32)
    query_acc, kv_grads = lax.fori_loop(0, turn_total, one_turn, (query_start, grads_start))
    query_low = (
        (query_acc * score_scale)
        .astype(jnp.bfloat16)
        .transpose(1, 2, 0, 3)
        .reshape(1, head_count * half_rows, col_width)
    )
    returned = lax.all_to_all(query_low, "head", split_axis=1, concat_axis=0, tiled=True)
    query_grad = (
        returned.reshape(group_count, 2, half_rows, col_width)
        .transpose(1, 2, 0, 3)
        .reshape(row_count, group_count * col_width)
    )
    flat_grads = kv_grads.transpose(1, 2, 0, 3).reshape(global_blocks * BLOCK, pair_width)
    summed = lax.psum_scatter(flat_grads, "region", scatter_dimension=0, tiled=True)
    kept_cols = lax.dynamic_slice_in_dim(summed, my_share * col_width, col_width, 1)
    given_cols = lax.dynamic_slice_in_dim(summed, (1 - my_share) * col_width, col_width, 1)
    kv_grad = kept_cols + from_partner(given_cols.astype(jnp.bfloat16), "head", 0).astype(
        given_cols.dtype
    )
    return (query_grad, kv_grad)


def solution(mesh):
    in_specs = (
        P(("region", "head"), None),
        P(("region", "head"), None),
        P(("region", "head"), None),
        P(None, "region"),
        P("region", None),
        P("region", None),
        P("region"),
    )
    out_specs = (P(("region", "head"), None), P("region", "head"))
    return jax.shard_map(body, mesh=mesh, in_specs=in_specs, out_specs=out_specs, check_vma=False)
```

profile of v0, /device:TPU:1, one launch (start us, length us, event | category | flops | bytes accessed | tf_op | source)
XLA Modules:
  0.0 470.4 jit_solution(11522040303615324225)
XLA Ops:
  10.8 14.5 %all-to-all-start.2 = ((f32[64,1,64]{2,1,0:T(1,128)}), f32[64,1,64]{2,1,0:T(1,128)S(1)}, u32[]{:S(2)}, u32[]{:S(2)}) async-start(f32[64,1,64]{2,1,0:T(1,128)} %bitcast.12), calls=%async_computation.2 | async-start | bytes 65536 | tf_op jit(solution)/shard_map/all_to_all | solution.py:72
  30.0 4.7 all-to-all-done.2
  34.7 6.0 %all-to-all-start = ((bf16[64,2,2048]{2,1,0:T(2,128)(2,1)}), bf16[64,2,2048]{2,1,0:T(2,128)(2,1)}, u32[]{:S(2)}, u32[]{:S(2)}) async-start(bf16[64,2,2048]{2,1,0:T(2,128)(2,1)} %reshape.267), calls=%async_computation | async-start | bytes 1048576 | tf_op jit(solution)/shard_map/all_to_all | solution.py:57
  45.4 12.5 %all-to-all-done = bf16[64,2,2048]{2,1,0:T(2,128)(2,1)} async-done(((bf16[64,2,2048]{2,1,0:T(2,128)(2,1)}), bf16[64,2,2048]{2,1,0:T(2,128)(2,1)}, u32[]{:S(2)}, u32[]{:S(2)}) %all-to-all-start) | async-done | bytes 524320 | tf_op jit(solution)/shard_map/all_to_all | solution.py:57
  57.9 6.5 %all-to-all-start.1 = ((bf16[64,2,2048]{2,1,0:T(2,128)(2,1)}), bf16[64,2,2048]{2,1,0:T(2,128)(2,1)}, u32[]{:S(2)}, u32[]{:S(2)}) async-start(bf16[64,2,2048]{2,1,0:T(2,128)(2,1)} %reshape.269), calls=%async_computation.1 | async-start | bytes 1048576 | tf_op jit(solution)/shard_map/all_to_all | solution.py:64
  67.9 27.4 %all_gather.3 = bf16[1536,128]{1,0:T(8,128)(2,1)S(1)} all-gather(bf16[128,128]{1,0:T(8,128)(2,1)S(1)} %constant_dynamic-slice_fusion.1), channel_id=1, replica_groups=mesh['region'=12,'head'=64] {'region'}, dimensions={0}, use_global_device_ids=true | all-gather | bytes 425984 | tf_op jit(solution)/shard_map/all_gather | solution.py:96
  106.3 264.2 %while.16 = (s32[]{:T(128)}, f32[1,64,64,64]{3,2,1,0:T(8,128)}, f32[1,24,64,128]{3,2,1,0:T(8,128)S(1)}, s32[64,8]{1,0:T(8,128)S(1)}, bf16[1,24,64,128]{3,2,1,0:T...) while((s32[]{:T(128)}, f32[1,64,64,64]{3,2,1,0:T(8,128)}, ...), condition=%wide.region_3.4_spmd.clone, body=%wide.region_1.3_spmd.clone.sunk | while | flops 342361728 | bytes 80980056 | solution.py:149
  124.8 5.6 %concatenate.17 = f32[1,64,2,64,64]{3,2,4,1,0:T(2,128)} reshape(f32[64,128,64]{1,2,0:T(8,128)} %fusion.26) | data formatting | bytes 4194304 | tf_op jit(solution)/shard_map/while/body/eval_jaxpr/concatenate | solution.py:141
  133.4 5.6 %concatenate.18 = f32[1,64,2,64,64]{3,2,4,1,0:T(2,128)} reshape(f32[64,128,64]{1,2,0:T(8,128)} %convolution_multiply_fusion.2) | data formatting | bytes 4194304 | tf_op jit(solution)/shard_map/while/body/eval_jaxpr/concatenate | solution.py:141
  139.1 8.5 %pad_maximum_fusion.2 = f32[1,64,2,64,128]{3,2,4,1,0:T(2,128)} fusion(f32[1,64,2,64,64]{3,2,4,1,0:T(2,128)} %concatenate.17, f32[1,64,2,64,64]{3,2,4,1,0:T(2,128)} %concatenate.18), kind=kLoop, calls=%fused_computation.2.clone.1 | loop fusion | flops 1048576 | bytes 8388608 | tf_op jit(solution)/shard_map/while/body/eval_jaxpr/concatenate | solution.py:141
  147.5 10.9 %copy.103 = f32[1,64,2,64,128]{4,3,2,1,0:T(8,128)} copy(f32[1,64,2,64,128]{3,2,4,1,0:T(2,128)} %pad_maximum_fusion.2) | data formatting | bytes 8388608 | tf_op jit(solution)/shard_map/while/body/eval_jaxpr/concatenate | solution.py:141
  158.4 13.5 %scatter_fusion = f32[24,64,128]{2,1,0:T(8,128)S(1)} fusion(f32[24,64,128]{2,1,0:T(8,128)S(1)} %bitcast.116, s32[128]{0:T(128)S(1)} %reshape.282, f32[128,64,128]{2,1,0:T(8,128)} %bitcast.122), kind=kCustom, calls=%fused_computation.1.clone.clone.1 | custom fusion | flops 1048576 | bytes 12583424 | tf_op jit(solution)/shard_map/while/body/eval_jaxpr/scatter-add | solution.py:144
  191.0 5.6 %concatenate.17 = f32[1,64,2,64,64]{3,2,4,1,0:T(2,128)} reshape(f32[64,128,64]{1,2,0:T(8,128)} %fusion.26) | data formatting | bytes 4194304 | tf_op jit(solution)/shard_map/while/body/eval_jaxpr/concatenate | solution.py:141
  199.6 5.6 %concatenate.18 = f32[1,64,2,64,64]{3,2,4,1,0:T(2,128)} reshape(f32[64,128,64]{1,2,0:T(8,128)} %convolution_multiply_fusion.2) | data formatting | bytes 4194304 | tf_op jit(solution)/shard_map/while/body/eval_jaxpr/concatenate | solution.py:141
  205.3 8.5 %pad_maximum_fusion.2 = f32[1,64,2,64,128]{3,2,4,1,0:T(2,128)} fusion(f32[1,64,2,64,64]{3,2,4,1,0:T(2,128)} %concatenate.17, f32[1,64,2,64,64]{3,2,4,1,0:T(2,128)} %concatenate.18), kind=kLoop, calls=%fused_computation.2.clone.1 | loop fusion | flops 1048576 | bytes 8388608 | tf_op jit(solution)/shard_map/while/body/eval_jaxpr/concatenate | solution.py:141
  213.7 10.9 %copy.103 = f32[1,64,2,64,128]{4,3,2,1,0:T(8,128)} copy(f32[1,64,2,64,128]{3,2,4,1,0:T(2,128)} %pad_maximum_fusion.2) | data formatting | bytes 8388608 | tf_op jit(solution)/shard_map/while/body/eval_jaxpr/concatenate | solution.py:141
  224.6 13.5 %scatter_fusion = f32[24,64,128]{2,1,0:T(8,128)S(1)} fusion(f32[24,64,128]{2,1,0:T(8,128)S(1)} %bitcast.116, s32[128]{0:T(128)S(1)} %reshape.282, f32[128,64,128]{2,1,0:T(8,128)} %bitcast.122), kind=kCustom, calls=%fused_computation.1.clone.clone.1 | custom fusion | flops 1048576 | bytes 12583424 | tf_op jit(solution)/shard_map/while/body/eval_jaxpr/scatter-add | solution.py:144
  257.2 5.6 %concatenate.17 = f32[1,64,2,64,64]{3,2,4,1,0:T(2,128)} reshape(f32[64,128,64]{1,2,0:T(8,128)} %fusion.26) | data formatting | bytes 4194304 | tf_op jit(solution)/shard_map/while/body/eval_jaxpr/concatenate | solution.py:141
  265.8 5.6 %concatenate.18 = f32[1,64,2,64,64]{3,2,4,1,0:T(2,128)} reshape(f32[64,128,64]{1,2,0:T(8,128)} %convolution_multiply_fusion.2) | data formatting | bytes 4194304 | tf_op jit(solution)/shard_map/while/body/eval_jaxpr/concatenate | solution.py:141
  271.5 8.5 %pad_maximum_fusion.2 = f32[1,64,2,64,128]{3,2,4,1,0:T(2,128)} fusion(f32[1,64,2,64,64]{3,2,4,1,0:T(2,128)} %concatenate.17, f32[1,64,2,64,64]{3,2,4,1,0:T(2,128)} %concatenate.18), kind=kLoop, calls=%fused_computation.2.clone.1 | loop fusion | flops 1048576 | bytes 8388608 | tf_op jit(solution)/shard_map/while/body/eval_jaxpr/concatenate | solution.py:141
  279.9 10.9 %copy.103 = f32[1,64,2,64,128]{4,3,2,1,0:T(8,128)} copy(f32[1,64,2,64,128]{3,2,4,1,0:T(2,128)} %pad_maximum_fusion.2) | data formatting | bytes 8388608 | tf_op jit(solution)/shard_map/while/body/eval_jaxpr/concatenate | solution.py:141
  290.8 13.5 %scatter_fusion = f32[24,64,128]{2,1,0:T(8,128)S(1)} fusion(f32[24,64,128]{2,1,0:T(8,128)S(1)} %bitcast.116, s32[128]{0:T(128)S(1)} %reshape.282, f32[128,64,128]{2,1,0:T(8,128)} %bitcast.122), kind=kCustom, calls=%fused_computation.1.clone.clone.1 | custom fusion | flops 1048576 | bytes 12583424 | tf_op jit(solution)/shard_map/while/body/eval_jaxpr/scatter-add | solution.py:144
  307.2 4.4 exponential_multiply_fusion.2
  323.4 5.6 %concatenate.17 = f32[1,64,2,64,64]{3,2,4,1,0:T(2,128)} reshape(f32[64,128,64]{1,2,0:T(8,128)} %fusion.26) | data formatting | bytes 4194304 | tf_op jit(solution)/shard_map/while/body/eval_jaxpr/concatenate | solution.py:141
  332.0 5.6 %concatenate.18 = f32[1,64,2,64,64]{3,2,4,1,0:T(2,128)} reshape(f32[64,128,64]{1,2,0:T(8,128)} %convolution_multiply_fusion.2) | data formatting | bytes 4194304 | tf_op jit(solution)/shard_map/while/body/eval_jaxpr/concatenate | solution.py:141
  337.7 8.5 %pad_maximum_fusion.2 = f32[1,64,2,64,128]{3,2,4,1,0:T(2,128)} fusion(f32[1,64,2,64,64]{3,2,4,1,0:T(2,128)} %concatenate.17, f32[1,64,2,64,64]{3,2,4,1,0:T(2,128)} %concatenate.18), kind=kLoop, calls=%fused_computation.2.clone.1 | loop fusion | flops 1048576 | bytes 8388608 | tf_op jit(solution)/shard_map/while/body/eval_jaxpr/concatenate | solution.py:141
  346.2 10.9 %copy.103 = f32[1,64,2,64,128]{4,3,2,1,0:T(8,128)} copy(f32[1,64,2,64,128]{3,2,4,1,0:T(2,128)} %pad_maximum_fusion.2) | data formatting | bytes 8388608 | tf_op jit(solution)/shard_map/while/body/eval_jaxpr/concatenate | solution.py:141
  357.0 13.5 %scatter_fusion = f32[24,64,128]{2,1,0:T(8,128)S(1)} fusion(f32[24,64,128]{2,1,0:T(8,128)S(1)} %bitcast.116, s32[128]{0:T(128)S(1)} %reshape.282, f32[128,64,128]{2,1,0:T(8,128)} %bitcast.122), kind=kCustom, calls=%fused_computation.1.clone.clone.1 | custom fusion | flops 1048576 | bytes 12583424 | tf_op jit(solution)/shard_map/while/body/eval_jaxpr/scatter-add | solution.py:144
  373.4 16.7 %copy.99 = bf16[1,4096,64]{2,0,1:T(2,128)(2,1)S(1)} copy(bf16[1,4096,64]{2,1,0:T(8,128)(2,1)S(1)} %bitcast.127) | data formatting | bytes 1048576 | tf_op jit(solution)/shard_map/reshape;transpose | solution.py:154
  390.6 23.6 %reduce.10 = bf16[4096,64]{1,0:T(8,128)(2,1)} reduce(bf16[4096,1,64]{2,1,0:T(2,128)(2,1)S(1)} %bitcast.126, bf16[]{:T(256)} %broadcast.103), dimensions={1}, to_apply=%bitcast.81.reduce_sub_computation | reduce | bytes 1048578
  417.2 14.7 %all-to-all-start.3 = ((bf16[64,2,2048]{2,1,0:T(2,128)(2,1)}), bf16[64,2,2048]{2,1,0:T(2,128)(2,1)}, u32[]{:S(2)}, u32[]{:S(2)}) async-start(bf16[64,2,2048]{2,1,0:T(2,128)(2,1)} %reshape.271), calls=%async_computation.3 | async-start | bytes 1048576 | tf_op jit(solution)/shard_map/all_to_all | solution.py:156
  435.3 13.8 %all-to-all-done.3 = bf16[64,2,2048]{2,1,0:T(2,128)(2,1)} async-done(((bf16[64,2,2048]{2,1,0:T(2,128)(2,1)}), bf16[64,2,2048]{2,1,0:T(2,128)(2,1)}, u32[]{:S(2)}, u32[]{:S(2)}) %all-to-all-start.3) | async-done | bytes 524320 | tf_op jit(solution)/shard_map/all_to_all | solution.py:156
  (152 shorter events, 134.4 us)
Async XLA Ops:
  7.2 60.6 %copy-start = (bf16[128,4096]{1,0:T(8,128)(2,1)S(1)}, bf16[128,4096]{1,0:T(8,128)(2,1)}, u32[]{:S(2)}) copy-start(bf16[128,4096]{1,0:T(8,128)(2,1)} %param.13) | copy-start | bytes 3145732
  10.8 23.9 %all-to-all-start.2 = ((f32[64,1,64]{2,1,0:T(1,128)}), f32[64,1,64]{2,1,0:T(1,128)S(1)}, u32[]{:S(2)}, u32[]{:S(2)}) async-start(f32[64,1,64]{2,1,0:T(1,128)} %bitcast.12), calls=%async_computation.2 | async-start | bytes 65536 | tf_op jit(solution)/shard_map/all_to_all | solution.py:72
  34.7 23.2 %all-to-all-start = ((bf16[64,2,2048]{2,1,0:T(2,128)(2,1)}), bf16[64,2,2048]{2,1,0:T(2,128)(2,1)}, u32[]{:S(2)}, u32[]{:S(2)}) async-start(bf16[64,2,2048]{2,1,0:T(2,128)(2,1)} %reshape.267), calls=%async_computation | async-start | bytes 1048576 | tf_op jit(solution)/shard_map/all_to_all | solution.py:57
  42.8 21.7 %copy-start.7 = (s32[128,8]{0,1:T(8,128)S(1)}, s32[128,8]{0,1:T(8,128)}, u32[]{:S(2)}) copy-start(s32[128,8]{0,1:T(8,128)} %param.14) | copy-start | bytes 12292
  45.4 22.0 %copy-start.8 = (s32[128]{0:T(128)S(1)}, s32[128]{0:T(128)}, u32[]{:S(2)}) copy-start(s32[128]{0:T(128)} %param.15) | copy-start | bytes 1540
  57.9 43.0 %all-to-all-start.1 = ((bf16[64,2,2048]{2,1,0:T(2,128)(2,1)}), bf16[64,2,2048]{2,1,0:T(2,128)(2,1)}, u32[]{:S(2)}, u32[]{:S(2)}) async-start(bf16[64,2,2048]{2,1,0:T(2,128)(2,1)} %reshape.269), calls=%async_computation.1 | async-start | bytes 1048576 | tf_op jit(solution)/shard_map/all_to_all | solution.py:64
  64.4 367.6 %reduce-scatter.2.cloned.1.call-start = ((), (), s32[]{:S(2)}) async-start(), calls=%async_computation.5 | async-start | bytes 851968 | tf_op jit(solution)/shard_map/reduce_scatter | solution.py:163
  106.4 2.8 copy-start.4
  119.3 3.8 copy-start.2
  119.3 3.8 copy-start.3
  158.4 13.5 %copy-start.5 = (bf16[1,64,64,64]{2,3,1,0:T(8,128)(2,1)S(1)}, bf16[1,64,64,64]{2,3,1,0:T(8,128)(2,1)}, u32[]{:S(2)}) copy-start(bf16[1,64,64,64]{2,3,1,0:T(8,128)(2,1)} %copy-done.4) | copy-start | bytes 1572868 | tf_op jit(solution)/shard_map/while
  171.9 2.8 copy-start.4
  184.8 4.4 copy-start.2
  184.9 4.4 copy-start.3
  224.6 13.5 %copy-start.5 = (bf16[1,64,64,64]{2,3,1,0:T(8,128)(2,1)S(1)}, bf16[1,64,64,64]{2,3,1,0:T(8,128)(2,1)}, u32[]{:S(2)}) copy-start(bf16[1,64,64,64]{2,3,1,0:T(8,128)(2,1)} %copy-done.4) | copy-start | bytes 1572868 | tf_op jit(solution)/shard_map/while
  238.1 2.8 copy-start.4
  251.0 4.4 copy-start.2
  251.1 4.4 copy-start.3
  290.8 13.5 %copy-start.5 = (bf16[1,64,64,64]{2,3,1,0:T(8,128)(2,1)S(1)}, bf16[1,64,64,64]{2,3,1,0:T(8,128)(2,1)}, u32[]{:S(2)}) copy-start(bf16[1,64,64,64]{2,3,1,0:T(8,128)(2,1)} %copy-done.4) | copy-start | bytes 1572868 | tf_op jit(solution)/shard_map/while
  304.3 2.8 copy-start.4
  317.3 4.4 copy-start.2
  317.3 4.4 copy-start.3
  357.0 13.5 %copy-start.5 = (bf16[1,64,64,64]{2,3,1,0:T(8,128)(2,1)S(1)}, bf16[1,64,64,64]{2,3,1,0:T(8,128)(2,1)}, u32[]{:S(2)}) copy-start(bf16[1,64,64,64]{2,3,1,0:T(8,128)(2,1)} %copy-done.4) | copy-start | bytes 1572868 | tf_op jit(solution)/shard_map/while
  370.6 0.9 copy-start.1
  417.2 31.9 %all-to-all-start.3 = ((bf16[64,2,2048]{2,1,0:T(2,128)(2,1)}), bf16[64,2,2048]{2,1,0:T(2,128)(2,1)}, u32[]{:S(2)}, u32[]{:S(2)}) async-start(bf16[64,2,2048]{2,1,0:T(2,128)(2,1)} %reshape.271), calls=%async_computation.3 | async-start | bytes 1048576 | tf_op jit(solution)/shard_map/all_to_all | solution.py:156
  432.9 29.9 %collective-permute-start = (bf16[128,64]{1,0:T(8,128)(2,1)S(1)}, bf16[128,64]{1,0:T(8,128)(2,1)S(1)}, u32[]{:S(2)}, u32[]{:S(2)}) collective-permute-start(bf16[128,64]{1,0:T(8,128)(2,1)S(1)} %dynamic-slice_convert_fusion), channel_id=1, source_target_pairs={{0,1},{1,0},{2,3},{3,2},{4,5},{5,4},{6,7},{7,6},{8,9},{9,8},{10,11... | collective-permute-start | bytes 49160 | tf_op jit(solution)/shard_map/ppermute | solution.py:20
  459.7 3.1 copy-start.6
Sparse Core Ops, SparseCore 0:
  371.6 48.3 reduce-scatter.1
where the time goes:
time: 475 us; the launch traced here: 470 us
  local copies, waits for them, and re-layouts  164 us (35%)
  other arithmetic  118 us (25%)
  matrix products  71.2 us (15%)
  starting transfers between devices  44.1 us (9%)
  waiting for transfers between devices  31.1 us (7%)
  blocking collectives  27.4 us (6%)
  between operations  14.4 us (3%)
    concatenate x12, local copies, waits for them, and re-layouts, one_turn(): jnp.concatenate([key_grad, value_grad], axis=-1)  88.5 us
    scatter-add x4, other arithmetic, one_turn(): kv_grads = kv_grads.at[:, pair_ids].add(pieces)  54 us
    concatenate x4, other arithmetic, one_turn(): jnp.concatenate([key_grad, value_grad], axis=-1)  33.9 us
    all_gather x1, blocking collectives, body(): kv_whole = lax.all_gather(kv_mine, 'region', axis=0, tiled=True)  27.4 us
    unnamed x2, other arithmetic  23.6 us
    unnamed x21, local copies, waits for them, and re-layouts  21.3 us
    dot_general x4, matrix products, one_turn(): jnp.einsum('hbtd,hbud->hbtu', query_heads, key_block, preferred_element_t...  17.7 us
    dot_general x4, matrix products, one_turn(): jnp.einsum('hbtd,hbud->hbtu', grad_heads, value_block, preferred_element_...  17.5 us
  transfers between devices with their start and end apart: 6, of which 3 were waited for; matrix products, arithmetic and copies ran while one was open for 17% of the time, Pallas kernels for 0%

commit v1 on v0

v1 whole, which is shorter than its diff:
```python
import jax
import jax.numpy as jnp
from jax import lax
from jax.experimental import pallas as pl
from jax.experimental.pallas import tpu as pltpu
from jax.sharding import Mesh, PartitionSpec as P

HEADS = 32
HD = 64
BLOCK = 64
SCALE = 0.125
GROUP = 4
UNROLL = 4
TAIL = 8
F32 = jnp.float32
BF16 = jnp.bfloat16


def lanes(shape):
    return lax.broadcasted_iota(jnp.int32, shape, len(shape) - 1)


def swap_halves(x):
    return pltpu.roll(x, HD, x.ndim - 1)


def pack_kernel(q_ref, g_ref, o_ref, x_ref):
    rows = q_ref.shape[0]
    width = q_ref.shape[1]
    low = lanes((rows, 128)) < HD
    row_head = lax.broadcasted_iota(jnp.int32, (HEADS, 128), 0)
    delta = jnp.zeros((HEADS, rows), F32)
    for pair in range(width // 128):
        cols = pl.ds(pair * 128, 128)
        q = q_ref[:, cols].astype(F32)
        g = g_ref[:, cols].astype(F32)
        first = jnp.where(low, q, swap_halves(g)).astype(BF16)
        second = jnp.where(low, swap_halves(q), g).astype(BF16)
        for share in range(2):
            part = slice(share * BLOCK, (share + 1) * BLOCK)
            x_ref[4 * pair + share, 0:BLOCK, :] = first[part]
            x_ref[4 * pair + 2 + share, 0:BLOCK, :] = second[part]
        product = g * o_ref[:, cols].astype(F32)
        high = product.astype(BF16)
        rest = (product - high.astype(F32)).astype(BF16)
        picks = (row_head == 2 * pair + lanes((HEADS, 128)) // HD).astype(BF16)
        dims = (((1,), (1,)), ((), ()))
        delta += lax.dot_general(picks, high, dims, preferred_element_type=F32)
        delta += lax.dot_general(picks, rest, dims, preferred_element_type=F32)
    high = delta.astype(BF16).astype(F32)
    rest = delta - high
    low = lanes((HEADS, 128)) < HD
    tails = (
        jnp.where(low, high, swap_halves(rest)),
        jnp.where(low, swap_halves(high), rest),
    )
    for head in range(HEADS):
        for share in range(2):
            row = jnp.broadcast_to(tails[share][head : head + 1], (TAIL, 128))
            x_ref[2 * head + share, BLOCK : BLOCK + TAIL, :] = row.astype(BF16)


def attention_kernel(
    ids_ref, counts_ref, share_ref, x_ref, norm_ref, kv_ref, dq_ref, dkv_ref, acc_ref, query_ref
):
    blocks = x_ref.shape[0]
    share = share_ref[0]
    low_row = lanes((1, 128)) < HD
    low = lanes((BLOCK, 128)) < HD
    half = lanes((128, 128)) < HD
    entry = lanes((1, GROUP * BLOCK)) // BLOCK

    def clear(index, carry):
        acc_ref[index] = jnp.zeros(acc_ref.shape[1:], F32)
        return carry

    lax.fori_loop(0, acc_ref.shape[0], clear, 0)

    def run_items(items, first_entry, fresh):
        staged = []
        for m in items:
            row = 2 * m + share
            count = counts_ref[row]
            ids = [ids_ref[row * 8 + first_entry + i] for i in range(GROUP)]
            x = x_ref[m, 0:BLOCK, :]
            tail = x_ref[m, BLOCK : BLOCK + TAIL, :].astype(F32)[0:1]
            delta = tail + swap_halves(tail)
            norm = norm_ref[pl.ds(m, 1), :]
            norm = jnp.where(share == 1, norm, swap_halves(norm))
            column = jnp.where(low_row, delta, norm)
            column = jnp.broadcast_to(column, (128, 128)).T
            xf = x.astype(F32)
            q_rows = jnp.where(low, xf * SCALE, 0.0)
            g_rows = jnp.where(low, 0.0, xf)
            stacked = jnp.concatenate([q_rows, g_rows], axis=0)
            left = stacked.astype(BF16)
            left_t = stacked.T.astype(BF16)
            keys = jnp.concatenate([kv_ref[i] for i in ids], axis=0)
            both = lax.dot_general(
                left, keys, (((1,), (1,)), ((), ())), preferred_element_type=F32
            )
            live = entry + first_entry < count
            staged.append((m, ids, column, left_t, keys, both, live))
        results = []
        for m, ids, column, left_t, keys, both, live in staged:
            wide = jnp.concatenate([column] * (GROUP // 2), axis=1)
            weights = jnp.where(live, jnp.exp(both[:BLOCK] - wide[BLOCK:]), 0.0)
            score_grad = (weights * (both[BLOCK:] - wide[:BLOCK])).astype(BF16)
            both_low = jnp.concatenate([score_grad, weights.astype(BF16)], axis=0)
            kv_part = jnp.dot(left_t, both_low, preferred_element_type=F32)
            query_part = jnp.dot(score_grad, keys, preferred_element_type=F32)
            results.append((m, ids, kv_part, query_part))
        for m, ids, kv_part, query_part in results:
            if fresh:
                query_ref[m] = query_part
            else:
                query_ref[m] = query_ref[m] + query_part
            for i in range(GROUP):
                tile = kv_part[:, (i // 2) * 128 : (i // 2) * 128 + 128]
                kept = jnp.where(half if i % 2 == 0 else ~half, tile, 0.0)
                acc_ref[ids[i]] = acc_ref[ids[i]] + kept

    def first_turn(step, carry):
        run_items([step * UNROLL + i for i in range(UNROLL)], 0, True)
        return carry

    lax.fori_loop(0, blocks // UNROLL, first_turn, 0)

    def second_turn(m, carry):
        @pl.when(counts_ref[2 * m + share] > GROUP)
        def _():
            run_items([m], GROUP, False)

        return carry

    lax.fori_loop(0, blocks, second_turn, 0)

    def finish_query(m, carry):
        grad = query_ref[m] * SCALE
        upper = swap_halves(grad[BLOCK // 2 :])
        dq_ref[m] = jnp.where(low[: BLOCK // 2], grad[: BLOCK // 2], upper).astype(BF16)
        return carry

    lax.fori_loop(0, blocks, finish_query, 0)

    def finish_kv(region, carry):
        first = acc_ref[2 * region]
        second = acc_ref[2 * region + 1]
        joined = jnp.where(half, first + swap_halves(first), second + swap_halves(second))
        joined = joined.astype(BF16)
        dkv_ref[2 * region] = joined[:HD]
        dkv_ref[2 * region + 1] = joined[HD:]
        return carry

    lax.fori_loop(0, acc_ref.shape[0] // 2, finish_kv, 0)


def unpack_kernel(y_ref, out_ref):
    half_rows = BLOCK // 2
    low = lanes((half_rows, 128)) < HD
    for pair in range(HEADS // 2):
        cols = pl.ds(pair * 128, 128)
        for share in range(2):
            first = y_ref[4 * pair + share].astype(F32)
            second = y_ref[4 * pair + 2 + share].astype(F32)
            base = share * BLOCK
            upper = jnp.where(low, first, swap_halves(second))
            lower = jnp.where(low, swap_halves(first), second)
            out_ref[base : base + half_rows, cols] = upper.astype(BF16)
            out_ref[base + half_rows : base + BLOCK, cols] = lower.astype(BF16)


def sum_kernel(parts_ref, out_ref):
    total = parts_ref[0].astype(F32)
    for i in range(1, parts_ref.shape[0]):
        total = total + parts_ref[i].astype(F32)
    out_ref[...] = total.T


def vmem(count):
    return [pl.BlockSpec(memory_space=pltpu.VMEM)] * count


def body(query, output, grad_out, log_norm, global_kv, block_ids, block_counts):
    members = ("chip", "core")
    chips = lax.axis_size("chip")
    cores = lax.axis_size("core")
    regions = lax.axis_size("region")
    member_count = chips * cores
    my_head = lax.axis_index("chip")
    my_share = lax.axis_index("core")
    blocks = block_ids.shape[0] // 2
    limit = pltpu.CompilerParams(vmem_limit_bytes=32 * 1024 * 1024)

    sent = pl.pallas_call(
        pack_kernel,
        out_shape=jax.ShapeDtypeStruct((member_count, BLOCK + TAIL, 128), BF16),
        in_specs=vmem(3),
        out_specs=vmem(1)[0],
        compiler_params=limit,
        name="pack",
    )(query, grad_out, output)
    received = lax.all_to_all(sent, members, split_axis=0, concat_axis=0, tiled=True)

    kv_mine = lax.dynamic_slice_in_dim(global_kv, my_head * 128, 128, 1)
    kv_whole = lax.all_gather(kv_mine, "region", axis=0, tiled=True)
    kv_blocks = kv_whole.reshape(-1, BLOCK, 2 * HD)
    norm_mine = lax.dynamic_slice_in_dim(log_norm, my_head, 1, 0).reshape(blocks, 128)
    smem = pl.BlockSpec(memory_space=pltpu.SMEM)
    global_blocks = kv_blocks.shape[0]
    dq, dkv = pl.pallas_call(
        attention_kernel,
        out_shape=(
            jax.ShapeDtypeStruct((blocks, BLOCK // 2, 128), BF16),
            jax.ShapeDtypeStruct((global_blocks, HD, 128), BF16),
        ),
        in_specs=[smem] * 3 + vmem(3),
        out_specs=tuple(vmem(2)),
        scratch_shapes=[
            pltpu.VMEM((global_blocks, 128, 128), F32),
            pltpu.VMEM((blocks, BLOCK, 128), F32),
        ],
        compiler_params=limit,
        name="attention",
    )(
        block_ids.reshape(-1),
        block_counts,
        my_share.reshape(1).astype(jnp.int32),
        received,
        norm_mine,
        kv_blocks,
    )
    returned = lax.all_to_all(dq, members, split_axis=0, concat_axis=0, tiled=True)
    parts = lax.all_to_all(dkv, ("region", "core"), split_axis=0, concat_axis=0, tiled=True)
    query_grad = pl.pallas_call(
        unpack_kernel,
        out_shape=jax.ShapeDtypeStruct(query.shape, BF16),
        in_specs=vmem(1),
        out_specs=vmem(1)[0],
        compiler_params=limit,
        name="unpack",
    )(returned)
    kv_grad = pl.pallas_call(
        sum_kernel,
        out_shape=jax.ShapeDtypeStruct((2 * BLOCK, HD), F32),
        in_specs=vmem(1),
        out_specs=vmem(1)[0],
        compiler_params=limit,
        name="sum_parts",
    )(parts)
    return (query_grad, kv_grad)


def solution(mesh):
    regions = mesh.shape["region"]
    devices = mesh.devices.reshape(regions, -1, 2)
    split = Mesh(devices, ("region", "chip", "core"))
    tokens = ("region", "chip", "core")
    in_specs = (
        P(tokens, None),
        P(tokens, None),
        P(tokens, None),
        P(None, "region"),
        P("region", None),
        P("region", None),
        P("region"),
    )
    out_specs = (P(tokens, None), P("region", ("chip", "core")))
    return jax.shard_map(body, mesh=split, in_specs=in_specs, out_specs=out_specs, check_vma=False)
```

time: 475 us -> 128 us (0.27)
  local copies, waits for them, and re-layouts: 164 us -> 5.1 us
  other arithmetic: 118 us -> 0 us
  matrix products: 71.2 us -> 0 us
  blocking collectives: 27.4 us -> 55.5 us
  Pallas kernels: 0 us -> 24.1 us
  starting transfers between devices: 44.1 us -> 21.3 us
  between operations: 14.4 us -> 0.71 us
  waiting for transfers between devices: 31.1 us -> 19.7 us
    concatenate x12 -> x0, local copies, waits for them, and re-layouts: 88.5 us -> none  [one_turn(): jnp.concatenate([key_grad, value_grad], axis=-1)]
    dot_general x20 -> x0, matrix products: 71.2 us -> none  [the longest x4 17.7 us: one_turn(): jnp.einsum('hbtd,hbud->hbtu', query_heads, key_block, preferred_element_t...]
    scatter-add x4 -> x0, other arithmetic: 54 us -> none  [one_turn(): kv_grads = kv_grads.at[:, pair_ids].add(pieces)]
    concatenate x4 -> x0, other arithmetic: 33.9 us -> none  [one_turn(): jnp.concatenate([key_grad, value_grad], axis=-1)]
    all_to_all x0 -> x1, blocking collectives: none -> 27.8 us  [body(): lax.all_to_all(dq, members, split_axis=0, concat_axis=0, tiled=True)]
    pallas_call x0 -> x4, Pallas kernels: none -> 24.1 us  [the longest x1 21.1 us: body(): pl.pallas_call(attention_kernel, out_shape=(jax.ShapeDtypeStruct((blocks,...]
    unnamed x2 -> x0, other arithmetic: 23.6 us -> none
    all_to_all x4 -> x2, starting transfers between devices: 41.7 us -> 21.3 us  [the longest x1 14.7 us: body(): lax.all_to_all(sent, members, split_axis=0, concat_axis=0, tiled=True)]
  transfers between devices with their start and end apart: 6 -> 2, of which waited for: 3 -> 2; matrix products, arithmetic and copies ran while one was open for 17% -> 1% of each run, Pallas kernels for 0% -> 1%
where the time goes in v1:
time: 128 us; the launch traced here: 126 us
  blocking collectives  55.5 us (43%)
  Pallas kernels  24.1 us (19%)
  starting transfers between devices  21.3 us (17%)
  waiting for transfers between devices  19.7 us (15%)
  local copies, waits for them, and re-layouts  5.1 us (4%)
    all_to_all x1, blocking collectives, body(): lax.all_to_all(dq, members, split_axis=0, concat_axis=0, tiled=True)  27.8 us
    all_gather x1, blocking collectives, body(): kv_whole = lax.all_gather(kv_mine, 'region', axis=0, tiled=True)  27.6 us
    pallas_call x1, Pallas kernels, body(): pl.pallas_call(attention_kernel, out_shape=(jax.ShapeDtypeStruct((blocks,...  21.1 us
    all_to_all x1, waiting for transfers between devices, body(): lax.all_to_all(dkv, ('region', 'core'), split_axis=0, concat_axis=0, tile...  17.2 us
    all_to_all x1, starting transfers between devices, body(): lax.all_to_all(sent, members, split_axis=0, concat_axis=0, tiled=True)  14.7 us
    all_to_all x1, starting transfers between devices, body(): lax.all_to_all(dkv, ('region', 'core'), split_axis=0, concat_axis=0, tile...  6.52 us
    unnamed x14, local copies, waits for them, and re-layouts  4.02 us
  transfers between devices with their start and end apart: 2, of which 2 were waited for; matrix products, arithmetic and copies ran while one was open for 1% of the time, Pallas kernels for 1%

profile of v1, /device:TPU:1, one launch (start us, length us, event | category | flops | bytes accessed | tf_op | source)
XLA Modules:
  0.0 126.3 jit_solution(9058701183465698187)
XLA Ops:
  0.6 0.0 copy-start
  0.6 0.0 copy-start.1
  0.7 1.1 copy-done.1
  1.8 0.0 copy-start.2
  1.8 1.0 copy-done.2
  2.8 0.0 copy-start.3
  2.8 1.0 copy-done.3
  3.9 1.9 %pack.1 = bf16[64,72,128]{2,1,0:T(8,128)(2,1)} custom-call(bf16[128,2048]{1,0:T(8,128)(2,1)S(1)} %copy-done.1, bf16[128,2048]{1,0:T(8,128)(2,1)S(1)} %copy-done.2, bf16[128,2048]{1,0:T(8,128)(2,1)S(1)} %copy-done.3), custom_call_target="tpu_custom_call" | custom-call | tf_op jit(solution)/shard_map/pack/pallas_call | solution.py:195
  5.7 0.0 copy-start.5
  5.7 0.0 copy-start.4
  5.7 14.7 %all-to-all-start = ((bf16[64,72,128]{2,1,0:T(8,128)(2,1)}), bf16[64,72,128]{2,1,0:T(8,128)(2,1)S(1)}, u32[]{:S(2)}, u32[]{:S(2)}) async-start(bf16[64,72,128]{2,1,0:T(8,128)(2,1)} %pack.1), calls=%async_computation | async-start | bytes 2359296 | tf_op jit(solution)/shard_map/all_to_all | solution.py:203
  20.5 0.0 copy-done.5
  20.5 0.1 copy.10
  20.6 0.1 reshape.16.ids_ref
  20.7 0.0 copy-done
  20.7 27.6 %all_gather.3 = bf16[1536,128]{1,0:T(8,128)(2,1)S(1)} all-gather(bf16[128,128]{1,0:T(8,128)(2,1)S(1)} %constant_dynamic-slice_fusion), channel_id=1, replica_groups=mesh['region'=12,'chip'=32,'core'=2] {'region'}, dimensions={0}, use_global_device_ids=true | all-gather | bytes 425984 | tf_op jit(solution)/shard_map/all_gather | solution.py:206
  48.4 1.0 constant_dynamic-slice_fusion.1
  49.3 2.5 %all-to-all-done.x_ref = bf16[64,72,128]{2,1,0:T(8,128)(2,1)S(1)} async-done(((bf16[64,72,128]{2,1,0:T(8,128)(2,1)}), bf16[64,72,128]{2,1,0:T(8,128)(2,1)S(1)}, u32[]{:S(2)}, u32[]{:S(2)}) %all-to-all-start) | async-done | bytes 1179680 | tf_op jit(solution)/shard_map/all_to_all | solution.py:203
  51.9 0.0 copy-done.4
  51.9 21.1 %attention.1 = (bf16[64,32,128]{2,1,0:T(8,128)(2,1)S(1)}, bf16[24,64,128]{2,1,0:T(8,128)(2,1)}) custom-call(s32[1024]{0:T(1024)S(1)} %reshape.16.ids_ref, s32[128]{0:T(128)S(1)} %copy-done.4, s32[1]{0:T(128)} %bitcast.share_ref, bf16[64,72,128]{2,1,0:T(8,128)(2,1)S(1)} %all-to-all-done.x_ref, f32[64,128]{1,0:T(8,128)S(1)} %bitcast.4, ...), custom_call_target="tpu_custom_call" | custom-call | tf_op jit(solution)/shard_map/attention/pallas_call | solution.py:211
  72.9 27.8 %all_to_all.15.y_ref = bf16[64,32,128]{2,1,0:T(8,128)(2,1)S(1)} all-to-all(bf16[64,32,128]{2,1,0:T(8,128)(2,1)S(1)} %get-tuple-element.4), channel_id=1, replica_groups=mesh['region'=12,'chip'=32,'core'=2] {'chip','core'}, dimensions={0} | all-to-all | bytes 1048576 | tf_op jit(solution)/shard_map/all_to_all | solution.py:233
  100.7 6.5 %all-to-all-start.2 = ((bf16[24,64,128]{2,1,0:T(8,128)(2,1)}), bf16[24,64,128]{2,1,0:T(8,128)(2,1)S(1)}, u32[]{:S(2)}, u32[]{:S(2)}) async-start(bf16[24,64,128]{2,1,0:T(8,128)(2,1)} %get-tuple-element.5), calls=%async_computation.2 | async-start | bytes 786432 | tf_op jit(solution)/shard_map/all_to_all | solution.py:234
  107.3 1.0 unpack.1
  108.3 17.2 %all-to-all-done.2.parts_ref = bf16[24,64,128]{2,1,0:T(8,128)(2,1)S(1)} async-done(((bf16[24,64,128]{2,1,0:T(8,128)(2,1)}), bf16[24,64,128]{2,1,0:T(8,128)(2,1)S(1)}, u32[]{:S(2)}, u32[]{:S(2)}) %all-to-all-start.2) | async-done | bytes 393248 | tf_op jit(solution)/shard_map/all_to_all | solution.py:234
  125.5 0.1 sum_parts.1
  125.6 0.7 copy.11
  (1 shorter events, 0.0 us)
Async XLA Ops:
  0.6 20.1 %copy-start = (bf16[128,4096]{1,0:T(8,128)(2,1)S(1)}, bf16[128,4096]{1,0:T(8,128)(2,1)}, u32[]{:S(2)}) copy-start(bf16[128,4096]{1,0:T(8,128)(2,1)} %param.11) | copy-start | bytes 3145732
  0.6 1.1 copy-start.1
  1.8 1.0 copy-start.2
  2.8 1.0 copy-start.3
  5.7 14.8 %copy-start.5 = (s32[128,8]{0,1:T(8,128)S(1)}, s32[128,8]{0,1:T(8,128)}, u32[]{:S(2)}) copy-start(s32[128,8]{0,1:T(8,128)} %param.12) | copy-start | bytes 12292
  5.7 46.1 %copy-start.4 = (s32[128]{0:T(128)S(1)}, s32[128]{0:T(128)}, u32[]{:S(2)}) copy-start(s32[128]{0:T(128)} %counts_ref.1) | copy-start | bytes 1540
  5.7 46.1 %all-to-all-start = ((bf16[64,72,128]{2,1,0:T(8,128)(2,1)}), bf16[64,72,128]{2,1,0:T(8,128)(2,1)S(1)}, u32[]{:S(2)}, u32[]{:S(2)}) async-start(bf16[64,72,128]{2,1,0:T(8,128)(2,1)} %pack.1), calls=%async_computation | async-start | bytes 2359296 | tf_op jit(solution)/shard_map/all_to_all | solution.py:203
  100.7 24.7 %all-to-all-start.2 = ((bf16[24,64,128]{2,1,0:T(8,128)(2,1)}), bf16[24,64,128]{2,1,0:T(8,128)(2,1)S(1)}, u32[]{:S(2)}, u32[]{:S(2)}) async-start(bf16[24,64,128]{2,1,0:T(8,128)(2,1)} %get-tuple-element.5), calls=%async_computation.2 | async-start | bytes 786432 | tf_op jit(solution)/shard_map/all_to_all | solution.py:234

commit v2 on v1

v2 whole, which is shorter than its diff:
```python
import jax
import jax.numpy as jnp
from jax import lax
from jax.experimental import pallas as pl
from jax.experimental.pallas import tpu as pltpu
from jax.sharding import Mesh, PartitionSpec as P

HEADS = 32
HD = 64
BLOCK = 64
SCALE = 0.125
GROUP = 4
UNROLL = 16
LATER_UNROLL = 8
PACK_STEPS = 4
TAIL = 8
F32 = jnp.float32
BF16 = jnp.bfloat16


def lanes(shape):
    return lax.broadcasted_iota(jnp.int32, shape, len(shape) - 1)


def swap_halves(x):
    return pltpu.roll(x, HD, x.ndim - 1)


def pack_kernel(q_ref, g_ref, o_ref, x_ref):
    rows, width = q_ref.shape
    heads = width // HD
    low = lanes((rows, 128)) < HD
    row_head = lax.broadcasted_iota(jnp.int32, (heads, 128), 0)
    delta = jnp.zeros((heads, rows), F32)
    for pair in range(heads // 2):
        cols = pl.ds(pair * 128, 128)
        q = q_ref[:, cols].astype(F32)
        g = g_ref[:, cols].astype(F32)
        first = jnp.where(low, q, swap_halves(g)).astype(BF16)
        second = jnp.where(low, swap_halves(q), g).astype(BF16)
        for share in range(2):
            part = slice(share * BLOCK, (share + 1) * BLOCK)
            x_ref[4 * pair + share, 0:BLOCK, :] = first[part]
            x_ref[4 * pair + 2 + share, 0:BLOCK, :] = second[part]
        product = g * o_ref[:, cols].astype(F32)
        high = product.astype(BF16)
        rest = (product - high.astype(F32)).astype(BF16)
        picks = (row_head == 2 * pair + lanes((heads, 128)) // HD).astype(BF16)
        dims = (((1,), (1,)), ((), ()))
        delta += lax.dot_general(picks, high, dims, preferred_element_type=F32)
        delta += lax.dot_general(picks, rest, dims, preferred_element_type=F32)
    high = delta.astype(BF16).astype(F32)
    rest = delta - high
    low = lanes((heads, 128)) < HD
    tails = (
        jnp.where(low, high, swap_halves(rest)),
        jnp.where(low, swap_halves(high), rest),
    )
    for head in range(heads):
        for share in range(2):
            row = jnp.broadcast_to(tails[share][head : head + 1], (TAIL, 128))
            x_ref[2 * head + share, BLOCK : BLOCK + TAIL, :] = row.astype(BF16)


def slot_of(region, my_region):
    ahead = lax.rem(region // 4 - my_region // 4 + 3, 3)
    low = lax.rem(region, 4) ^ lax.rem(my_region, 4)
    return lax.rem(low, 2) * 6 + low // 2 * 3 + ahead


def attention_kernel(
    ids_ref,
    counts_ref,
    place_ref,
    x_ref,
    norm_ref,
    kv_ref,
    dq_ref,
    kept_ref,
    given_ref,
    acc_ref,
    query_ref,
    later_ref,
):
    blocks = x_ref.shape[0]
    share = place_ref[0]
    my_region = place_ref[1]
    low_row = lanes((1, 128)) < HD
    low = lanes((BLOCK, 128)) < HD
    entry = lanes((1, GROUP * BLOCK)) // BLOCK

    def clear(index, carry):
        acc_ref[index] = jnp.zeros(acc_ref.shape[1:], F32)
        return carry

    lax.fori_loop(0, acc_ref.shape[0], clear, 0, unroll=4)

    def run_items(items, first_entry, fresh):
        staged = []
        for m, count in items:
            row = 2 * m + share
            ids = [ids_ref[first_entry + i, row] for i in range(GROUP)]
            tail = x_ref[m, BLOCK : BLOCK + TAIL, :].astype(F32)[0:1]
            delta = tail + swap_halves(tail)
            norm = norm_ref[pl.ds(m, 1), :]
            norm = jnp.where(share == 1, norm, swap_halves(norm))
            column = jnp.where(low_row, delta, norm)
            column = jnp.broadcast_to(column, (128, 128)).T
            x = x_ref[m, 0:BLOCK, :]
            zero = jnp.zeros_like(x)
            scaled = jnp.where(low, x * jnp.bfloat16(SCALE), zero)
            left = jnp.concatenate([scaled, jnp.where(low, zero, x)], axis=0)
            keys = jnp.concatenate([kv_ref[i] for i in ids], axis=0)
            both = lax.dot_general(
                left, keys, (((1,), (1,)), ((), ())), preferred_element_type=F32
            )
            live = entry + first_entry < count
            staged.append((m, ids, column, left, keys, both, live))
        results = []
        for m, ids, column, left, keys, both, live in staged:
            wide = jnp.concatenate([column] * (GROUP // 2), axis=1)
            weights = jnp.where(live, jnp.exp(both[:BLOCK] - wide[BLOCK:]), 0.0)
            score_grad = weights * (both[BLOCK:] - wide[:BLOCK])
            score_low = score_grad.astype(BF16)
            both_low = jnp.concatenate([score_low, weights.astype(BF16)], axis=0)
            kv_part = lax.dot_general(
                both_low, left, (((0,), (0,)), ((), ())), preferred_element_type=F32
            )
            query_part = jnp.dot(score_low, keys, preferred_element_type=F32)
            results.append((m, ids, kv_part, query_part))
        for m, ids, kv_part, query_part in results:
            if fresh:
                query_ref[m] = query_part
            else:
                query_ref[m] = query_ref[m] + query_part
            for i in range(GROUP):
                acc_ref[ids[i]] = acc_ref[ids[i]] + kv_part[i * BLOCK : (i + 1) * BLOCK]

    def first_turn(step, carry):
        base = step * UNROLL
        run_items([(base + i, counts_ref[2 * (base + i) + share]) for i in range(UNROLL)], 0, True)
        return carry

    lax.fori_loop(0, blocks // UNROLL, first_turn, 0)

    def note(m, found):
        later_ref[found] = m
        return found + (counts_ref[2 * m + share] > GROUP).astype(jnp.int32)

    later = lax.fori_loop(0, blocks, note, 0, unroll=8)

    def second_turn(step, carry):
        items = []
        for i in range(LATER_UNROLL):
            place = step * LATER_UNROLL + i
            m = later_ref[jnp.minimum(place, blocks - 1)]
            m = jnp.where(place < later, m, 0)
            items.append((m, jnp.where(place < later, counts_ref[2 * m + share], 0)))
        run_items(items, GROUP, False)
        return carry

    lax.fori_loop(0, (later + LATER_UNROLL - 1) // LATER_UNROLL, second_turn, 0)

    def finish_query(m, carry):
        grad = query_ref[m] * SCALE
        upper = swap_halves(grad[BLOCK // 2 :])
        dq_ref[m] = jnp.where(low[: BLOCK // 2], grad[: BLOCK // 2], upper).astype(BF16)
        return carry

    lax.fori_loop(0, blocks, finish_query, 0, unroll=8)

    def finish_kv(region, carry):
        first = acc_ref[2 * region]
        second = acc_ref[2 * region + 1]
        joined = jnp.concatenate([first, second], axis=0).T
        slot = slot_of(region, my_region)
        kept_ref[slot] = jnp.where(share == 0, joined[:HD], joined[HD:])
        given_ref[slot] = jnp.where(share == 0, joined[HD:], joined[:HD]).astype(BF16)
        return carry

    lax.fori_loop(0, acc_ref.shape[0] // 2, finish_kv, 0, unroll=4)


def unpack_kernel(y_ref, out_ref):
    half_rows = BLOCK // 2
    low = lanes((half_rows, 128)) < HD
    for pair in range(HEADS // 2):
        cols = pl.ds(pair * 128, 128)
        for share in range(2):
            first = y_ref[4 * pair + share].astype(F32)
            second = y_ref[4 * pair + 2 + share].astype(F32)
            base = share * BLOCK
            upper = jnp.where(low, first, swap_halves(second))
            lower = jnp.where(low, swap_halves(first), second)
            out_ref[base : base + half_rows, cols] = upper.astype(BF16)
            out_ref[base + half_rows : base + BLOCK, cols] = lower.astype(BF16)


def vmem(count):
    return [pl.BlockSpec(memory_space=pltpu.VMEM)] * count


def attention_call(ids, counts, place, received, norm, kv_blocks):
    blocks = received.shape[0]
    global_blocks = kv_blocks.shape[0]
    smem = pl.BlockSpec(memory_space=pltpu.SMEM)
    return pl.pallas_call(
        attention_kernel,
        out_shape=(
            jax.ShapeDtypeStruct((blocks, BLOCK // 2, 128), BF16),
            jax.ShapeDtypeStruct((global_blocks // 2, HD, 128), F32),
            jax.ShapeDtypeStruct((global_blocks // 2, HD, 128), BF16),
        ),
        in_specs=[smem] * 3 + vmem(3),
        out_specs=tuple(vmem(3)),
        scratch_shapes=[
            pltpu.VMEM((global_blocks, BLOCK, 128), F32),
            pltpu.VMEM((blocks, BLOCK, 128), F32),
            pltpu.SMEM((blocks + 1,), jnp.int32),
        ],
        compiler_params=pltpu.CompilerParams(vmem_limit_bytes=32 * 1024 * 1024),
        name="attention",
    )(ids, counts, place, received, norm, kv_blocks)


def body(query, output, grad_out, log_norm, global_kv, block_ids, block_counts):
    members = ("chip", "core")
    chips = lax.axis_size("chip")
    cores = lax.axis_size("core")
    regions = lax.axis_size("region")
    member_count = chips * cores
    my_head = lax.axis_index("chip")
    my_share = lax.axis_index("core")
    blocks = block_ids.shape[0] // 2
    limit = pltpu.CompilerParams(vmem_limit_bytes=32 * 1024 * 1024)

    rows, width = query.shape
    piece = pl.BlockSpec((rows, width // PACK_STEPS), lambda i: (0, i))
    sent = pl.pallas_call(
        pack_kernel,
        grid=(PACK_STEPS,),
        out_shape=jax.ShapeDtypeStruct((member_count, BLOCK + TAIL, 128), BF16),
        in_specs=[piece] * 3,
        out_specs=pl.BlockSpec(
            (member_count // PACK_STEPS, BLOCK + TAIL, 128), lambda i: (i, 0, 0)
        ),
        compiler_params=pltpu.CompilerParams(vmem_limit_bytes=60 * 1024 * 1024),
        name="pack",
    )(query, grad_out, output)
    received = lax.all_to_all(sent, members, split_axis=0, concat_axis=0, tiled=True)

    kv_mine = lax.dynamic_slice_in_dim(global_kv, my_head * 128, 128, 1)
    kv_whole = lax.all_gather(kv_mine, "region", axis=0, tiled=True)
    kv_blocks = kv_whole.reshape(-1, BLOCK, 2 * HD)
    norm_mine = lax.dynamic_slice_in_dim(log_norm, my_head, 1, 0).reshape(blocks, 128)
    dq, kept, given = attention_call(
        block_ids.T,
        block_counts,
        jnp.stack([my_share, lax.axis_index("region")]).astype(jnp.int32),
        received,
        norm_mine,
        kv_blocks,
    )
    returned = lax.all_to_all(dq, members, split_axis=0, concat_axis=0, tiled=True)
    taken = lax.ppermute(given, "core", [(0, 1), (1, 0)])
    chip_part = kept + taken.astype(F32)
    route = [(i, i ^ 1) for i in range(regions)]
    piece = lax.ppermute(chip_part[6:].astype(BF16), "region", route)
    half_part = chip_part[:6] + piece.astype(F32)
    route = [(i, i ^ 2) for i in range(regions)]
    piece = lax.ppermute(half_part[3:].astype(BF16), "region", route)
    line_part = half_part[:3] + piece.astype(F32)
    far = []
    for k in (1, 2):
        route = [(i, (i + 4 * k) % regions) for i in range(regions)]
        far.append(lax.ppermute(line_part[k].astype(BF16), "region", route))
    kv_grad = line_part[0]
    for piece in far:
        kv_grad = kv_grad + piece.astype(F32)
    query_grad = pl.pallas_call(
        unpack_kernel,
        out_shape=jax.ShapeDtypeStruct(query.shape, BF16),
        in_specs=vmem(1),
        out_specs=vmem(1)[0],
        compiler_params=limit,
        name="unpack",
    )(returned)
    return (query_grad, kv_grad.T)


def solution(mesh):
    regions = mesh.shape["region"]
    devices = mesh.devices.reshape(regions, -1, 2)
    split = Mesh(devices, ("region", "chip", "core"))
    tokens = ("region", "chip", "core")
    in_specs = (
        P(tokens, None),
        P(tokens, None),
        P(tokens, None),
        P(None, "region"),
        P("region", None),
        P("region", None),
        P("region"),
    )
    out_specs = (P(tokens, None), P("region", ("chip", "core")))
    return jax.shard_map(body, mesh=split, in_specs=in_specs, out_specs=out_specs, check_vma=False)
```

time: 128 us -> 104 us (0.81)
  blocking collectives: 55.5 us -> 27.5 us
  starting transfers between devices: 21.3 us -> 42.9 us
  Pallas kernels: 24.1 us -> 14.7 us
  waiting for transfers between devices: 19.7 us -> 14.5 us
  local copies, waits for them, and re-layouts: 5.1 us -> 1.03 us
    all_to_all x1 -> x0, blocking collectives: 27.8 us -> none  [body(): lax.all_to_all(dq, members, split_axis=0, concat_axis=0, tiled=True)]
    ppermute x0 -> x5, starting transfers between devices: none -> 17.8 us  [the longest x2 10.4 us: body(): far.append(lax.ppermute(line_part[k].astype(BF16), 'region', route))]
    all_to_all x1, waiting for transfers between devices: 17.2 us -> 0.01 us  [body(): lax.all_to_all(dq, members, split_axis=0, concat_axis=0, tiled=True)]
    ppermute x0 -> x5, waiting for transfers between devices: none -> 11.8 us  [the longest x2 6.61 us: body(): far.append(lax.ppermute(line_part[k].astype(BF16), 'region', route))]
    pallas_call x3 -> x2, Pallas kernels: 23.1 us -> 13.6 us  [the longest x1 9.36 us: attention_call(): pl.pallas_call(attention_kernel, out_shape=(jax.ShapeDtypeStruct((blocks,...]
    unnamed x14 -> x6, local copies, waits for them, and re-layouts: 4.02 us -> 0.02 us
    all_to_all x1, starting transfers between devices: 6.52 us -> 10.4 us  [body(): lax.all_to_all(dq, members, split_axis=0, concat_axis=0, tiled=True)]
  transfers between devices with their start and end apart: 2 -> 7, of which waited for: 2 -> 4; matrix products, arithmetic and copies ran while one was open for 1% -> 2% of each run, Pallas kernels for 1% -> 0%
where the time goes in v2:
time: 104 us; the launch traced here: 102 us
  starting transfers between devices  42.9 us (41%)
  blocking collectives  27.5 us (26%)
  Pallas kernels  14.7 us (14%)
  waiting for transfers between devices  14.5 us (14%)
    all_gather x1, blocking collectives, body(): kv_whole = lax.all_gather(kv_mine, 'region', axis=0, tiled=True)  27.5 us
    all_to_all x1, starting transfers between devices, body(): lax.all_to_all(sent, members, split_axis=0, concat_axis=0, tiled=True)  14.7 us
    all_to_all x1, starting transfers between devices, body(): lax.all_to_all(dq, members, split_axis=0, concat_axis=0, tiled=True)  10.4 us
    ppermute x2, starting transfers between devices, body(): far.append(lax.ppermute(line_part[k].astype(BF16), 'region', route))  10.4 us
    pallas_call x1, Pallas kernels, attention_call(): pl.pallas_call(attention_kernel, out_shape=(jax.ShapeDtypeStruct((blocks,...  9.36 us
    ppermute x2, waiting for transfers between devices, body(): far.append(lax.ppermute(line_part[k].astype(BF16), 'region', route))  6.61 us
    pallas_call x1, Pallas kernels, body(): pl.pallas_call(pack_kernel, grid=(PACK_STEPS,), out_shape=jax.ShapeDtypeS...  4.28 us
    ppermute x1, waiting for transfers between devices, body(): piece = lax.ppermute(half_part[3:].astype(BF16), 'region', route)  4.1 us
  transfers between devices with their start and end apart: 7, of which 4 were waited for; matrix products, arithmetic and copies ran while one was open for 2% of the time, Pallas kernels for 0%

profile of v2, /device:TPU:1, one launch (start us, length us, event | category | flops | bytes accessed | tf_op | source)
XLA Modules:
  0.0 102.2 jit_solution(8671778577461934180)
XLA Ops:
  0.6 0.0 copy-start
  0.6 4.3 %pack.1 = bf16[64,72,128]{2,1,0:T(8,128)(2,1)} custom-call(bf16[128,2048]{1,0:T(8,128)(2,1)} %q_ref.1, bf16[128,2048]{1,0:T(8,128)(2,1)} %g_ref.1, bf16[128,2048]{1,0:T(8,128)(2,1)} %o_ref.1), custom_call_target="tpu_custom_call" | custom-call | tf_op jit(solution)/shard_map/pack/pallas_call | solution.py:239
  4.9 0.0 copy-start.1
  4.9 0.0 copy-start.2
  4.9 14.7 %all-to-all-start = ((bf16[64,72,128]{2,1,0:T(8,128)(2,1)}), bf16[64,72,128]{2,1,0:T(8,128)(2,1)S(1)}, u32[]{:S(2)}, u32[]{:S(2)}) async-start(bf16[64,72,128]{2,1,0:T(8,128)(2,1)} %pack.1), calls=%async_computation | async-start | bytes 2359296 | tf_op jit(solution)/shard_map/all_to_all | solution.py:250
  19.7 0.1 pad_add_fusion.place_ref
  19.8 0.0 copy-done
  19.8 27.5 %all_gather.3 = bf16[1536,128]{1,0:T(8,128)(2,1)S(1)} all-gather(bf16[128,128]{1,0:T(8,128)(2,1)S(1)} %constant_dynamic-slice_fusion), channel_id=1, replica_groups=mesh['region'=12,'chip'=32,'core'=2] {'region'}, dimensions={0}, use_global_device_ids=true | all-gather | bytes 425984 | tf_op jit(solution)/shard_map/all_gather | solution.py:253
  47.3 1.0 constant_dynamic-slice_fusion.1
  48.3 2.8 %all-to-all-done.x_ref = bf16[64,72,128]{2,1,0:T(8,128)(2,1)S(1)} async-done(((bf16[64,72,128]{2,1,0:T(8,128)(2,1)}), bf16[64,72,128]{2,1,0:T(8,128)(2,1)S(1)}, u32[]{:S(2)}, u32[]{:S(2)}) %all-to-all-start) | async-done | bytes 1179680 | tf_op jit(solution)/shard_map/all_to_all | solution.py:250
  51.1 0.0 copy-done.1
  51.1 0.0 copy-done.2
  51.1 9.4 %attention.1 = (bf16[64,32,128]{2,1,0:T(8,128)(2,1)}, f32[12,64,128]{2,1,0:T(8,128)S(1)}, bf16[12,64,128]{2,1,0:T(8,128)(2,1)S(1)}) custom-call(s32[8,128]{1,0:T(8,128)S(1)} %bitcast.21, s32[128]{0:T(128)S(1)} %copy-done.2, s32[2]{0:T(128)S(1)} %pad_add_fusion.place_ref, bf16[64,72,128]{2,1,0:T(8,128)(2,1)S(1)} %all-to-all-done.x_ref, ...), custom_call_target="tpu_custom_call" | custom-call | tf_op jit(solution)/shard_map/attention/pallas_call | solution.py:207
  60.4 3.6 %collective-permute-start = (bf16[12,64,128]{2,1,0:T(8,128)(2,1)S(1)}, bf16[12,64,128]{2,1,0:T(8,128)(2,1)S(1)}, u32[]{:S(2)}, u32[]{:S(2)}) collective-permute-start(bf16[12,64,128]{2,1,0:T(8,128)(2,1)S(1)} %get-tuple-element.7), channel_id=1, source_target_pairs={{0,1},{1,0},{2,3},{3,2},{4,5},{5,4},{6,7},{7,6},{8,9},{9,8},{10,11... | collective-permute-start | bytes 589832 | tf_op jit(solution)/shard_map/ppermute | solution.py:265
  64.0 1.0 %collective-permute-done = bf16[12,64,128]{2,1,0:T(8,128)(2,1)S(1)} collective-permute-done((bf16[12,64,128]{2,1,0:T(8,128)(2,1)S(1)}, bf16[12,64,128]{2,1,0:T(8,128)(2,1)S(1)}, u32[]{:S(2)}, u32[]{:S(2)}) %collective-permute-start) | collective-permute-done | bytes 196640 | tf_op jit(solution)/shard_map/ppermute | solution.py:265
  65.2 1.9 %collective-permute-start.1 = (bf16[6,64,128]{2,1,0:T(8,128)(2,1)S(1)}, bf16[6,64,128]{2,1,0:T(8,128)(2,1)S(1)}, u32[]{:S(2)}, u32[]{:S(2)}) collective-permute-start(bf16[6,64,128]{2,1,0:T(8,128)(2,1)S(1)} %slice.52), channel_id=1, source_target_pairs={{0,64},{64,0},{128,192},{192,128},{256,320},{320,256},{384,448},{4... | collective-permute-start | bytes 294920 | tf_op jit(solution)/shard_map/ppermute | solution.py:268
  67.1 10.4 %all-to-all-start.1 = ((bf16[64,32,128]{2,1,0:T(8,128)(2,1)}), bf16[64,32,128]{2,1,0:T(8,128)(2,1)S(1)}, u32[]{:S(2)}, u32[]{:S(2)}) async-start(bf16[64,32,128]{2,1,0:T(8,128)(2,1)} %get-tuple-element.5), calls=%async_computation.1 | async-start | bytes 1048576 | tf_op jit(solution)/shard_map/all_to_all | solution.py:264
  77.4 0.0 collective-permute-done.1
  77.5 1.9 %collective-permute-start.2 = (bf16[3,64,128]{2,1,0:T(8,128)(2,1)S(1)}, bf16[3,64,128]{2,1,0:T(8,128)(2,1)S(1)}, u32[]{:S(2)}, u32[]{:S(2)}) collective-permute-start(bf16[3,64,128]{2,1,0:T(8,128)(2,1)S(1)} %slice.53), channel_id=1, source_target_pairs={{0,128},{64,192},{128,0},{192,64},{256,384},{320,448},{384,256},{4... | collective-permute-start | bytes 147464 | tf_op jit(solution)/shard_map/ppermute | solution.py:271
  79.4 4.1 %collective-permute-done.2 = bf16[3,64,128]{2,1,0:T(8,128)(2,1)S(1)} collective-permute-done((bf16[3,64,128]{2,1,0:T(8,128)(2,1)S(1)}, bf16[3,64,128]{2,1,0:T(8,128)(2,1)S(1)}, u32[]{:S(2)}, u32[]{:S(2)}) %collective-permute-start.2) | collective-permute-done | bytes 49184 | tf_op jit(solution)/shard_map/ppermute | solution.py:271
  83.6 8.4 %collective-permute-start.4 = (bf16[64,128]{1,0:T(8,128)(2,1)S(1)}, bf16[64,128]{1,0:T(8,128)(2,1)S(1)}, u32[]{:S(2)}, u32[]{:S(2)}) collective-permute-start(bf16[64,128]{1,0:T(8,128)(2,1)S(1)} %get-tuple-element.11), channel_id=1, source_target_pairs={{0,512},{64,576},{128,640},{192,704},{256,0},{320,64},{384,128},{4... | collective-permute-start | bytes 49160 | tf_op jit(solution)/shard_map/ppermute | solution.py:276
  92.0 1.9 %collective-permute-start.3 = (bf16[64,128]{1,0:T(8,128)(2,1)S(1)}, bf16[64,128]{1,0:T(8,128)(2,1)S(1)}, u32[]{:S(2)}, u32[]{:S(2)}) collective-permute-start(bf16[64,128]{1,0:T(8,128)(2,1)S(1)} %get-tuple-element.10), channel_id=1, source_target_pairs={{0,256},{64,320},{128,384},{192,448},{256,512},{320,576},{384,640}... | collective-permute-start | bytes 49160 | tf_op jit(solution)/shard_map/ppermute | solution.py:276
  93.9 0.0 collective-permute-done.4
  93.9 6.6 %collective-permute-done.3 = bf16[64,128]{1,0:T(8,128)(2,1)S(1)} collective-permute-done((bf16[64,128]{1,0:T(8,128)(2,1)S(1)}, bf16[64,128]{1,0:T(8,128)(2,1)S(1)}, u32[]{:S(2)}, u32[]{:S(2)}) %collective-permute-start.3) | collective-permute-done | bytes 16416 | tf_op jit(solution)/shard_map/ppermute | solution.py:276
  100.5 0.6 fusion.2
  101.2 0.0 all-to-all-done.1.y_ref
  101.2 1.0 %unpack.1 = bf16[128,2048]{1,0:T(8,128)(2,1)} custom-call(bf16[64,32,128]{2,1,0:T(8,128)(2,1)S(1)} %all-to-all-done.1.y_ref), custom_call_target="tpu_custom_call" | custom-call | tf_op jit(solution)/shard_map/unpack/pallas_call | solution.py:280
  (7 shorter events, 0.1 us)
Async XLA Ops:
  0.6 19.1 %copy-start = (bf16[128,4096]{1,0:T(8,128)(2,1)S(1)}, bf16[128,4096]{1,0:T(8,128)(2,1)}, u32[]{:S(2)}) copy-start(bf16[128,4096]{1,0:T(8,128)(2,1)} %param.11) | copy-start | bytes 3145732
  4.9 46.1 %copy-start.1 = (s32[128,8]{0,1:T(8,128)S(1)}, s32[128,8]{0,1:T(8,128)}, u32[]{:S(2)}) copy-start(s32[128,8]{0,1:T(8,128)} %param.12) | copy-start | bytes 12292
  4.9 46.1 %copy-start.2 = (s32[128]{0:T(128)S(1)}, s32[128]{0:T(128)}, u32[]{:S(2)}) copy-start(s32[128]{0:T(128)} %counts_ref.1) | copy-start | bytes 1540
  4.9 46.1 %all-to-all-start = ((bf16[64,72,128]{2,1,0:T(8,128)(2,1)}), bf16[64,72,128]{2,1,0:T(8,128)(2,1)S(1)}, u32[]{:S(2)}, u32[]{:S(2)}) async-start(bf16[64,72,128]{2,1,0:T(8,128)(2,1)} %pack.1), calls=%async_computation | async-start | bytes 2359296 | tf_op jit(solution)/shard_map/all_to_all | solution.py:250
  60.4 4.7 %collective-permute-start = (bf16[12,64,128]{2,1,0:T(8,128)(2,1)S(1)}, bf16[12,64,128]{2,1,0:T(8,128)(2,1)S(1)}, u32[]{:S(2)}, u32[]{:S(2)}) collective-permute-start(bf16[12,64,128]{2,1,0:T(8,128)(2,1)S(1)} %get-tuple-element.7), channel_id=1, source_target_pairs={{0,1},{1,0},{2,3},{3,2},{4,5},{5,4},{6,7},{7,6},{8,9},{9,8},{10,11... | collective-permute-start | bytes 589832 | tf_op jit(solution)/shard_map/ppermute | solution.py:265
  65.2 12.3 %collective-permute-start.1 = (bf16[6,64,128]{2,1,0:T(8,128)(2,1)S(1)}, bf16[6,64,128]{2,1,0:T(8,128)(2,1)S(1)}, u32[]{:S(2)}, u32[]{:S(2)}) collective-permute-start(bf16[6,64,128]{2,1,0:T(8,128)(2,1)S(1)} %slice.52), channel_id=1, source_target_pairs={{0,64},{64,0},{128,192},{192,128},{256,320},{320,256},{384,448},{4... | collective-permute-start | bytes 294920 | tf_op jit(solution)/shard_map/ppermute | solution.py:268
  67.1 34.1 %all-to-all-start.1 = ((bf16[64,32,128]{2,1,0:T(8,128)(2,1)}), bf16[64,32,128]{2,1,0:T(8,128)(2,1)S(1)}, u32[]{:S(2)}, u32[]{:S(2)}) async-start(bf16[64,32,128]{2,1,0:T(8,128)(2,1)} %get-tuple-element.5), calls=%async_computation.1 | async-start | bytes 1048576 | tf_op jit(solution)/shard_map/all_to_all | solution.py:264
  77.5 6.0 %collective-permute-start.2 = (bf16[3,64,128]{2,1,0:T(8,128)(2,1)S(1)}, bf16[3,64,128]{2,1,0:T(8,128)(2,1)S(1)}, u32[]{:S(2)}, u32[]{:S(2)}) collective-permute-start(bf16[3,64,128]{2,1,0:T(8,128)(2,1)S(1)} %slice.53), channel_id=1, source_target_pairs={{0,128},{64,192},{128,0},{192,64},{256,384},{320,448},{384,256},{4... | collective-permute-start | bytes 147464 | tf_op jit(solution)/shard_map/ppermute | solution.py:271
  83.6 10.4 %collective-permute-start.4 = (bf16[64,128]{1,0:T(8,128)(2,1)S(1)}, bf16[64,128]{1,0:T(8,128)(2,1)S(1)}, u32[]{:S(2)}, u32[]{:S(2)}) collective-permute-start(bf16[64,128]{1,0:T(8,128)(2,1)S(1)} %get-tuple-element.11), channel_id=1, source_target_pairs={{0,512},{64,576},{128,640},{192,704},{256,0},{320,64},{384,128},{4... | collective-permute-start | bytes 49160 | tf_op jit(solution)/shard_map/ppermute | solution.py:276
  92.0 8.5 %collective-permute-start.3 = (bf16[64,128]{1,0:T(8,128)(2,1)S(1)}, bf16[64,128]{1,0:T(8,128)(2,1)S(1)}, u32[]{:S(2)}, u32[]{:S(2)}) collective-permute-start(bf16[64,128]{1,0:T(8,128)(2,1)S(1)} %get-tuple-element.10), channel_id=1, source_target_pairs={{0,256},{64,320},{128,384},{192,448},{256,512},{320,576},{384,640}... | collective-permute-start | bytes 49160 | tf_op jit(solution)/shard_map/ppermute | solution.py:276

commit v3 on v2

--- a/solution.py
+++ b/solution.py
@@ -10,9 +10,9 @@
 BLOCK = 64
 SCALE = 0.125
 GROUP = 4
-UNROLL = 16
+UNROLL = 32
 LATER_UNROLL = 8
-PACK_STEPS = 4
+PACK_STEPS = 2
 TAIL = 8
 F32 = jnp.float32
 BF16 = jnp.bfloat16
@@ -129,10 +129,12 @@
             query_part = jnp.dot(score_low, keys, preferred_element_type=F32)
             results.append((m, ids, kv_part, query_part))
         for m, ids, kv_part, query_part in results:
-            if fresh:
-                query_ref[m] = query_part
-            else:
-                query_ref[m] = query_ref[m] + query_part
+            if not fresh:
+                query_part = query_ref[m] + query_part
+            query_ref[m] = query_part
+            grad = query_part * SCALE
+            upper = swap_halves(grad[BLOCK // 2 :])
+            dq_ref[m] = jnp.where(low[: BLOCK // 2], grad[: BLOCK // 2], upper).astype(BF16)
             for i in range(GROUP):
                 acc_ref[ids[i]] = acc_ref[ids[i]] + kv_part[i * BLOCK : (i + 1) * BLOCK]
 
@@ -160,14 +162,6 @@
         return carry
 
     lax.fori_loop(0, (later + LATER_UNROLL - 1) // LATER_UNROLL, second_turn, 0)
-
-    def finish_query(m, carry):
-        grad = query_ref[m] * SCALE
-        upper = swap_halves(grad[BLOCK // 2 :])
-        dq_ref[m] = jnp.where(low[: BLOCK // 2], grad[: BLOCK // 2], upper).astype(BF16)
-        return carry
-
-    lax.fori_loop(0, blocks, finish_query, 0, unroll=8)
 
     def finish_kv(region, carry):
         first = acc_ref[2 * region]
@@ -198,6 +192,22 @@
 
 def vmem(count):
     return [pl.BlockSpec(memory_space=pltpu.VMEM)] * count
+
+
+def pack_call(query, grad_out, output):
+    rows, width = query.shape
+    piece = pl.BlockSpec((rows, width // PACK_STEPS), lambda i: (0, i))
+    return pl.pallas_call(
+        pack_kernel,
+        grid=(PACK_STEPS,),
+        out_shape=jax.ShapeDtypeStruct((2 * HEADS, BLOCK + TAIL, 128), BF16),
+        in_specs=[piece] * 3,
+        out_specs=pl.BlockSpec(
+            (2 * HEADS // PACK_STEPS, BLOCK + TAIL, 128), lambda i: (i, 0, 0)
+        ),
+        compiler_params=pltpu.CompilerParams(vmem_limit_bytes=60 * 1024 * 1024),
+        name="pack",
+    )(query, grad_out, output)
 
 
 def attention_call(ids, counts, place, received, norm, kv_blocks):
@@ -234,19 +244,7 @@
     blocks = block_ids.shape[0] // 2
     limit = pltpu.CompilerParams(vmem_limit_bytes=32 * 1024 * 1024)
 
-    rows, width = query.shape
-    piece = pl.BlockSpec((rows, width // PACK_STEPS), lambda i: (0, i))
-    sent = pl.pallas_call(
-        pack_kernel,
-        grid=(PACK_STEPS,),
-        out_shape=jax.ShapeDtypeStruct((member_count, BLOCK + TAIL, 128), BF16),
-        in_specs=[piece] * 3,
-        out_specs=pl.BlockSpec(
-            (member_count // PACK_STEPS, BLOCK + TAIL, 128), lambda i: (i, 0, 0)
-        ),
-        compiler_params=pltpu.CompilerParams(vmem_limit_bytes=60 * 1024 * 1024),
-        name="pack",
-    )(query, grad_out, output)
+    sent = pack_call(query, grad_out, output)
     received = lax.all_to_all(sent, members, split_axis=0, concat_axis=0, tiled=True)
 
     kv_mine = lax.dynamic_slice_in_dim(global_kv, my_head * 128, 128, 1)

time: 104 us -> 101 us (0.971)
  Pallas kernels: 14.7 us -> 11.5 us
    pallas_call x1, Pallas kernels: 9.36 us -> 7.42 us  [attention_call(): pl.pallas_call(attention_kernel, out_shape=(jax.ShapeDtypeStruct((blocks,...]
    pallas_call x1, Pallas kernels: 4.28 us -> 3.02 us  [pack_call(): pl.pallas_call(pack_kernel, grid=(PACK_STEPS,), out_shape=jax.ShapeDtypeS...]
where the time goes in v3:
time: 101 us; the launch traced here: 100 us
  starting transfers between devices  43.7 us (43%)
  blocking collectives  27.5 us (27%)
  waiting for transfers between devices  14.6 us (14%)
  Pallas kernels  11.5 us (11%)
  local copies, waits for them, and re-layouts  1.03 us (1%)
    all_gather x1, blocking collectives, body(): kv_whole = lax.all_gather(kv_mine, 'region', axis=0, tiled=True)  27.5 us
    all_to_all x1, starting transfers between devices, body(): lax.all_to_all(sent, members, split_axis=0, concat_axis=0, tiled=True)  14.7 us
    ppermute x2, starting transfers between devices, body(): far.append(lax.ppermute(line_part[k].astype(BF16), 'region', route))  10.4 us
    all_to_all x1, starting transfers between devices, body(): lax.all_to_all(dq, members, split_axis=0, concat_axis=0, tiled=True)  10.3 us
    pallas_call x1, Pallas kernels, attention_call(): pl.pallas_call(attention_kernel, out_shape=(jax.ShapeDtypeStruct((blocks,...  7.42 us
    ppermute x2, waiting for transfers between devices, body(): far.append(lax.ppermute(line_part[k].astype(BF16), 'region', route))  6.73 us
    ppermute x1, starting transfers between devices, body(): taken = lax.ppermute(given, 'core', [(0, 1), (1, 0)])  4.43 us
    ppermute x1, waiting for transfers between devices, body(): piece = lax.ppermute(half_part[3:].astype(BF16), 'region', route)  4.1 us
  transfers between devices with their start and end apart: 7, of which 4 were waited for; matrix products, arithmetic and copies ran while one was open for 2% of the time, Pallas kernels for 0%

profile of v3, /device:TPU:1, one launch (start us, length us, event | category | flops | bytes accessed | tf_op | source)
XLA Modules:
  0.0 100.0 jit_solution(10007655594476382095)
XLA Ops:
  0.6 0.0 copy-start
  0.6 3.0 %pack.1 = bf16[64,72,128]{2,1,0:T(8,128)(2,1)} custom-call(bf16[128,2048]{1,0:T(8,128)(2,1)} %q_ref.1, bf16[128,2048]{1,0:T(8,128)(2,1)} %g_ref.1, bf16[128,2048]{1,0:T(8,128)(2,1)} %o_ref.1), custom_call_target="tpu_custom_call" | custom-call | tf_op jit(solution)/shard_map/pack/pallas_call | solution.py:200
  3.7 0.0 copy-start.1
  3.7 0.0 copy-start.2
  3.7 14.7 %all-to-all-start = ((bf16[64,72,128]{2,1,0:T(8,128)(2,1)}), bf16[64,72,128]{2,1,0:T(8,128)(2,1)S(1)}, u32[]{:S(2)}, u32[]{:S(2)}) async-start(bf16[64,72,128]{2,1,0:T(8,128)(2,1)} %pack.1), calls=%async_computation | async-start | bytes 2359296 | tf_op jit(solution)/shard_map/all_to_all | solution.py:248
  18.4 0.1 pad_add_fusion.place_ref
  18.5 0.0 copy-done
  18.5 27.5 %all_gather.3 = bf16[1536,128]{1,0:T(8,128)(2,1)S(1)} all-gather(bf16[128,128]{1,0:T(8,128)(2,1)S(1)} %constant_dynamic-slice_fusion), channel_id=1, replica_groups=mesh['region'=12,'chip'=32,'core'=2] {'region'}, dimensions={0}, use_global_device_ids=true | all-gather | bytes 425984 | tf_op jit(solution)/shard_map/all_gather | solution.py:251
  46.1 1.0 constant_dynamic-slice_fusion.1
  47.0 2.8 %all-to-all-done.x_ref = bf16[64,72,128]{2,1,0:T(8,128)(2,1)S(1)} async-done(((bf16[64,72,128]{2,1,0:T(8,128)(2,1)}), bf16[64,72,128]{2,1,0:T(8,128)(2,1)S(1)}, u32[]{:S(2)}, u32[]{:S(2)}) %all-to-all-start) | async-done | bytes 1179680 | tf_op jit(solution)/shard_map/all_to_all | solution.py:248
  49.8 0.0 copy-done.1
  49.8 0.0 copy-done.2
  49.8 7.4 %attention.1 = (bf16[64,32,128]{2,1,0:T(8,128)(2,1)}, f32[12,64,128]{2,1,0:T(8,128)S(1)}, bf16[12,64,128]{2,1,0:T(8,128)(2,1)S(1)}) custom-call(s32[8,128]{1,0:T(8,128)S(1)} %bitcast.21, s32[128]{0:T(128)S(1)} %copy-done.2, s32[2]{0:T(128)S(1)} %pad_add_fusion.place_ref, bf16[64,72,128]{2,1,0:T(8,128)(2,1)S(1)} %all-to-all-done.x_ref, ...), custom_call_target="tpu_custom_call" | custom-call | tf_op jit(solution)/shard_map/attention/pallas_call | solution.py:217
  57.2 4.4 %collective-permute-start = (bf16[12,64,128]{2,1,0:T(8,128)(2,1)S(1)}, bf16[12,64,128]{2,1,0:T(8,128)(2,1)S(1)}, u32[]{:S(2)}, u32[]{:S(2)}) collective-permute-start(bf16[12,64,128]{2,1,0:T(8,128)(2,1)S(1)} %get-tuple-element.7), channel_id=1, source_target_pairs={{0,1},{1,0},{2,3},{3,2},{4,5},{5,4},{6,7},{7,6},{8,9},{9,8},{10,11... | collective-permute-start | bytes 589832 | tf_op jit(solution)/shard_map/ppermute | solution.py:263
  61.7 1.0 %collective-permute-done = bf16[12,64,128]{2,1,0:T(8,128)(2,1)S(1)} collective-permute-done((bf16[12,64,128]{2,1,0:T(8,128)(2,1)S(1)}, bf16[12,64,128]{2,1,0:T(8,128)(2,1)S(1)}, u32[]{:S(2)}, u32[]{:S(2)}) %collective-permute-start) | collective-permute-done | bytes 196640 | tf_op jit(solution)/shard_map/ppermute | solution.py:263
  62.8 1.9 %collective-permute-start.1 = (bf16[6,64,128]{2,1,0:T(8,128)(2,1)S(1)}, bf16[6,64,128]{2,1,0:T(8,128)(2,1)S(1)}, u32[]{:S(2)}, u32[]{:S(2)}) collective-permute-start(bf16[6,64,128]{2,1,0:T(8,128)(2,1)S(1)} %slice.52), channel_id=1, source_target_pairs={{0,64},{64,0},{128,192},{192,128},{256,320},{320,256},{384,448},{4... | collective-permute-start | bytes 294920 | tf_op jit(solution)/shard_map/ppermute | solution.py:266
  64.7 10.3 %all-to-all-start.1 = ((bf16[64,32,128]{2,1,0:T(8,128)(2,1)}), bf16[64,32,128]{2,1,0:T(8,128)(2,1)S(1)}, u32[]{:S(2)}, u32[]{:S(2)}) async-start(bf16[64,32,128]{2,1,0:T(8,128)(2,1)} %get-tuple-element.5), calls=%async_computation.1 | async-start | bytes 1048576 | tf_op jit(solution)/shard_map/all_to_all | solution.py:262
  75.1 0.0 collective-permute-done.1
  75.1 1.9 %collective-permute-start.2 = (bf16[3,64,128]{2,1,0:T(8,128)(2,1)S(1)}, bf16[3,64,128]{2,1,0:T(8,128)(2,1)S(1)}, u32[]{:S(2)}, u32[]{:S(2)}) collective-permute-start(bf16[3,64,128]{2,1,0:T(8,128)(2,1)S(1)} %slice.53), channel_id=1, source_target_pairs={{0,128},{64,192},{128,0},{192,64},{256,384},{320,448},{384,256},{4... | collective-permute-start | bytes 147464 | tf_op jit(solution)/shard_map/ppermute | solution.py:269
  77.1 4.1 %collective-permute-done.2 = bf16[3,64,128]{2,1,0:T(8,128)(2,1)S(1)} collective-permute-done((bf16[3,64,128]{2,1,0:T(8,128)(2,1)S(1)}, bf16[3,64,128]{2,1,0:T(8,128)(2,1)S(1)}, u32[]{:S(2)}, u32[]{:S(2)}) %collective-permute-start.2) | collective-permute-done | bytes 49184 | tf_op jit(solution)/shard_map/ppermute | solution.py:269
  81.2 8.4 %collective-permute-start.4 = (bf16[64,128]{1,0:T(8,128)(2,1)S(1)}, bf16[64,128]{1,0:T(8,128)(2,1)S(1)}, u32[]{:S(2)}, u32[]{:S(2)}) collective-permute-start(bf16[64,128]{1,0:T(8,128)(2,1)S(1)} %get-tuple-element.11), channel_id=1, source_target_pairs={{0,512},{64,576},{128,640},{192,704},{256,0},{320,64},{384,128},{4... | collective-permute-start | bytes 49160 | tf_op jit(solution)/shard_map/ppermute | solution.py:274
  89.6 1.9 %collective-permute-start.3 = (bf16[64,128]{1,0:T(8,128)(2,1)S(1)}, bf16[64,128]{1,0:T(8,128)(2,1)S(1)}, u32[]{:S(2)}, u32[]{:S(2)}) collective-permute-start(bf16[64,128]{1,0:T(8,128)(2,1)S(1)} %get-tuple-element.10), channel_id=1, source_target_pairs={{0,256},{64,320},{128,384},{192,448},{256,512},{320,576},{384,640}... | collective-permute-start | bytes 49160 | tf_op jit(solution)/shard_map/ppermute | solution.py:274
  91.6 0.0 collective-permute-done.4
  91.6 6.7 %collective-permute-done.3 = bf16[64,128]{1,0:T(8,128)(2,1)S(1)} collective-permute-done((bf16[64,128]{1,0:T(8,128)(2,1)S(1)}, bf16[64,128]{1,0:T(8,128)(2,1)S(1)}, u32[]{:S(2)}, u32[]{:S(2)}) %collective-permute-start.3) | collective-permute-done | bytes 16416 | tf_op jit(solution)/shard_map/ppermute | solution.py:274
  98.3 0.6 fusion.2
  98.9 0.0 all-to-all-done.1.y_ref
  98.9 1.0 %unpack.1 = bf16[128,2048]{1,0:T(8,128)(2,1)} custom-call(bf16[64,32,128]{2,1,0:T(8,128)(2,1)S(1)} %all-to-all-done.1.y_ref), custom_call_target="tpu_custom_call" | custom-call | tf_op jit(solution)/shard_map/unpack/pallas_call | solution.py:278
  (7 shorter events, 0.1 us)
Async XLA Ops:
  0.6 17.9 %copy-start = (bf16[128,4096]{1,0:T(8,128)(2,1)S(1)}, bf16[128,4096]{1,0:T(8,128)(2,1)}, u32[]{:S(2)}) copy-start(bf16[128,4096]{1,0:T(8,128)(2,1)} %param.11) | copy-start | bytes 3145732
  3.7 46.1 %copy-start.1 = (s32[128,8]{0,1:T(8,128)S(1)}, s32[128,8]{0,1:T(8,128)}, u32[]{:S(2)}) copy-start(s32[128,8]{0,1:T(8,128)} %param.12) | copy-start | bytes 12292
  3.7 46.1 %copy-start.2 = (s32[128]{0:T(128)S(1)}, s32[128]{0:T(128)}, u32[]{:S(2)}) copy-start(s32[128]{0:T(128)} %counts_ref.1) | copy-start | bytes 1540
  3.7 46.1 %all-to-all-start = ((bf16[64,72,128]{2,1,0:T(8,128)(2,1)}), bf16[64,72,128]{2,1,0:T(8,128)(2,1)S(1)}, u32[]{:S(2)}, u32[]{:S(2)}) async-start(bf16[64,72,128]{2,1,0:T(8,128)(2,1)} %pack.1), calls=%async_computation | async-start | bytes 2359296 | tf_op jit(solution)/shard_map/all_to_all | solution.py:248
  57.2 5.5 %collective-permute-start = (bf16[12,64,128]{2,1,0:T(8,128)(2,1)S(1)}, bf16[12,64,128]{2,1,0:T(8,128)(2,1)S(1)}, u32[]{:S(2)}, u32[]{:S(2)}) collective-permute-start(bf16[12,64,128]{2,1,0:T(8,128)(2,1)S(1)} %get-tuple-element.7), channel_id=1, source_target_pairs={{0,1},{1,0},{2,3},{3,2},{4,5},{5,4},{6,7},{7,6},{8,9},{9,8},{10,11... | collective-permute-start | bytes 589832 | tf_op jit(solution)/shard_map/ppermute | solution.py:263
  62.8 12.3 %collective-permute-start.1 = (bf16[6,64,128]{2,1,0:T(8,128)(2,1)S(1)}, bf16[6,64,128]{2,1,0:T(8,128)(2,1)S(1)}, u32[]{:S(2)}, u32[]{:S(2)}) collective-permute-start(bf16[6,64,128]{2,1,0:T(8,128)(2,1)S(1)} %slice.52), channel_id=1, source_target_pairs={{0,64},{64,0},{128,192},{192,128},{256,320},{320,256},{384,448},{4... | collective-permute-start | bytes 294920 | tf_op jit(solution)/shard_map/ppermute | solution.py:266
  64.7 34.2 %all-to-all-start.1 = ((bf16[64,32,128]{2,1,0:T(8,128)(2,1)}), bf16[64,32,128]{2,1,0:T(8,128)(2,1)S(1)}, u32[]{:S(2)}, u32[]{:S(2)}) async-start(bf16[64,32,128]{2,1,0:T(8,128)(2,1)} %get-tuple-element.5), calls=%async_computation.1 | async-start | bytes 1048576 | tf_op jit(solution)/shard_map/all_to_all | solution.py:262
  75.1 6.0 %collective-permute-start.2 = (bf16[3,64,128]{2,1,0:T(8,128)(2,1)S(1)}, bf16[3,64,128]{2,1,0:T(8,128)(2,1)S(1)}, u32[]{:S(2)}, u32[]{:S(2)}) collective-permute-start(bf16[3,64,128]{2,1,0:T(8,128)(2,1)S(1)} %slice.53), channel_id=1, source_target_pairs={{0,128},{64,192},{128,0},{192,64},{256,384},{320,448},{384,256},{4... | collective-permute-start | bytes 147464 | tf_op jit(solution)/shard_map/ppermute | solution.py:269
  81.2 10.4 %collective-permute-start.4 = (bf16[64,128]{1,0:T(8,128)(2,1)S(1)}, bf16[64,128]{1,0:T(8,128)(2,1)S(1)}, u32[]{:S(2)}, u32[]{:S(2)}) collective-permute-start(bf16[64,128]{1,0:T(8,128)(2,1)S(1)} %get-tuple-element.11), channel_id=1, source_target_pairs={{0,512},{64,576},{128,640},{192,704},{256,0},{320,64},{384,128},{4... | collective-permute-start | bytes 49160 | tf_op jit(solution)/shard_map/ppermute | solution.py:274
  89.6 8.7 %collective-permute-start.3 = (bf16[64,128]{1,0:T(8,128)(2,1)S(1)}, bf16[64,128]{1,0:T(8,128)(2,1)S(1)}, u32[]{:S(2)}, u32[]{:S(2)}) collective-permute-start(bf16[64,128]{1,0:T(8,128)(2,1)S(1)} %get-tuple-element.10), channel_id=1, source_target_pairs={{0,256},{64,320},{128,384},{192,448},{256,512},{320,576},{384,640}... | collective-permute-start | bytes 49160 | tf_op jit(solution)/shard_map/ppermute | solution.py:274

commit v4 on v3

--- a/solution.py
+++ b/solution.py
@@ -16,6 +16,7 @@
 TAIL = 8
 F32 = jnp.float32
 BF16 = jnp.bfloat16
+REGION = ("third", "hop", "step")
 
 
 def lanes(shape):
@@ -62,10 +63,8 @@
             x_ref[2 * head + share, BLOCK : BLOCK + TAIL, :] = row.astype(BF16)
 
 
-def slot_of(region, my_region):
-    ahead = lax.rem(region // 4 - my_region // 4 + 3, 3)
-    low = lax.rem(region, 4) ^ lax.rem(my_region, 4)
-    return lax.rem(low, 2) * 6 + low // 2 * 3 + ahead
+def slot_of(line, my_region):
+    return (lax.rem(line, 2) ^ lax.rem(my_region // 2, 2)) * 3 + line // 2
 
 
 def attention_kernel(
@@ -163,16 +162,23 @@
 
     lax.fori_loop(0, (later + LATER_UNROLL - 1) // LATER_UNROLL, second_turn, 0)
 
-    def finish_kv(region, carry):
-        first = acc_ref[2 * region]
-        second = acc_ref[2 * region + 1]
-        joined = jnp.concatenate([first, second], axis=0).T
-        slot = slot_of(region, my_region)
-        kept_ref[slot] = jnp.where(share == 0, joined[:HD], joined[HD:])
-        given_ref[slot] = jnp.where(share == 0, joined[HD:], joined[:HD]).astype(BF16)
+    def finish_kv(line, carry):
+        slot = slot_of(line, my_region)
+        lines = acc_ref.shape[0] // 4
+        for other in range(2):
+            region = 2 * line + (lax.rem(my_region, 2) ^ other)
+            joined = jnp.concatenate([acc_ref[2 * region], acc_ref[2 * region + 1]], axis=0).T
+            own_half = jnp.where(share == 0, joined[:HD], joined[HD:])
+            other_half = jnp.where(share == 0, joined[HD:], joined[:HD])
+            if other == 0:
+                kept_ref[slot] = own_half
+                kept_ref[lines + slot] = other_half
+            else:
+                given_ref[slot] = own_half.astype(BF16)
+                given_ref[lines + slot] = other_half.astype(BF16)
         return carry
 
-    lax.fori_loop(0, acc_ref.shape[0] // 2, finish_kv, 0, unroll=4)
+    lax.fori_loop(0, acc_ref.shape[0] // 4, finish_kv, 0, unroll=2)
 
 
 def unpack_kernel(y_ref, out_ref):
@@ -237,7 +243,7 @@
     members = ("chip", "core")
     chips = lax.axis_size("chip")
     cores = lax.axis_size("core")
-    regions = lax.axis_size("region")
+    regions = lax.axis_size(REGION)
     member_count = chips * cores
     my_head = lax.axis_index("chip")
     my_share = lax.axis_index("core")
@@ -248,33 +254,29 @@
     received = lax.all_to_all(sent, members, split_axis=0, concat_axis=0, tiled=True)
 
     kv_mine = lax.dynamic_slice_in_dim(global_kv, my_head * 128, 128, 1)
-    kv_whole = lax.all_gather(kv_mine, "region", axis=0, tiled=True)
+    kv_whole = lax.all_gather(kv_mine, REGION, axis=0, tiled=True)
     kv_blocks = kv_whole.reshape(-1, BLOCK, 2 * HD)
     norm_mine = lax.dynamic_slice_in_dim(log_norm, my_head, 1, 0).reshape(blocks, 128)
     dq, kept, given = attention_call(
         block_ids.T,
         block_counts,
-        jnp.stack([my_share, lax.axis_index("region")]).astype(jnp.int32),
+        jnp.stack([my_share, lax.axis_index(REGION)]).astype(jnp.int32),
         received,
         norm_mine,
         kv_blocks,
     )
     returned = lax.all_to_all(dq, members, split_axis=0, concat_axis=0, tiled=True)
-    taken = lax.ppermute(given, "core", [(0, 1), (1, 0)])
-    chip_part = kept + taken.astype(F32)
-    route = [(i, i ^ 1) for i in range(regions)]
-    piece = lax.ppermute(chip_part[6:].astype(BF16), "region", route)
-    half_part = chip_part[:6] + piece.astype(F32)
-    route = [(i, i ^ 2) for i in range(regions)]
-    piece = lax.ppermute(half_part[3:].astype(BF16), "region", route)
-    line_part = half_part[:3] + piece.astype(F32)
-    far = []
-    for k in (1, 2):
-        route = [(i, (i + 4 * k) % regions) for i in range(regions)]
-        far.append(lax.ppermute(line_part[k].astype(BF16), "region", route))
-    kv_grad = line_part[0]
-    for piece in far:
-        kv_grad = kv_grad + piece.astype(F32)
+    swap = [(0, 1), (1, 0)]
+    piece = lax.ppermute(given, "step", swap)
+    step_part = kept + piece.astype(F32)
+    lines = regions // 2
+    piece = lax.ppermute(step_part[lines:].astype(BF16), "core", swap)
+    chip_part = step_part[:lines] + piece.astype(F32)
+    piece = lax.ppermute(chip_part[lines // 2 :].astype(BF16), "hop", swap)
+    hop_part = (chip_part[: lines // 2] + piece.astype(F32)).astype(BF16)
+    parts = lax.all_gather(hop_part, "third", axis=0, tiled=False)
+    mine = lax.dynamic_index_in_dim(parts, lax.axis_index("third"), axis=1, keepdims=False)
+    kv_grad = jnp.sum(mine.astype(F32), axis=0)
     query_grad = pl.pallas_call(
         unpack_kernel,
         out_shape=jax.ShapeDtypeStruct(query.shape, BF16),
@@ -288,17 +290,17 @@
 
 def solution(mesh):
     regions = mesh.shape["region"]
-    devices = mesh.devices.reshape(regions, -1, 2)
-    split = Mesh(devices, ("region", "chip", "core"))
-    tokens = ("region", "chip", "core")
+    devices = mesh.devices.reshape(regions // 4, 2, 2, -1, 2)
+    split = Mesh(devices, (*REGION, "chip", "core"))
+    tokens = (*REGION, "chip", "core")
     in_specs = (
         P(tokens, None),
         P(tokens, None),
         P(tokens, None),
-        P(None, "region"),
-        P("region", None),
-        P("region", None),
-        P("region"),
+        P(None, REGION),
+        P(REGION, None),
+        P(REGION, None),
+        P(REGION),
     )
-    out_specs = (P(tokens, None), P("region", ("chip", "core")))
+    out_specs = (P(tokens, None), P(REGION, ("chip", "core")))
     return jax.shard_map(body, mesh=split, in_specs=in_specs, out_specs=out_specs, check_vma=False)

time: 101 us -> 100 us (0.990)
  blocking collectives: 27.5 us -> 44.2 us
  starting transfers between devices: 43.7 us -> 32.6 us
  waiting for transfers between devices: 14.6 us -> 7.04 us
    all_gather x1 -> x2, blocking collectives: 27.5 us -> 44.2 us  [the longest x1 27.5 us: body(): kv_whole = lax.all_gather(kv_mine, REGION, axis=0, tiled=True)]
    ppermute x5 -> x3, starting transfers between devices: 18.6 us -> 6.95 us  [the longest x1 2.68 us: body(): piece = lax.ppermute(chip_part[lines // 2:].astype(BF16), 'hop', swap)]
    ppermute x5 -> x3, waiting for transfers between devices: 11.9 us -> 4.27 us  [the longest x1 3.34 us: body(): piece = lax.ppermute(chip_part[lines // 2:].astype(BF16), 'hop', swap)]
  transfers between devices with their start and end apart: 7 -> 5, of which waited for: 4 -> 3; matrix products, arithmetic and copies ran while one was open for 2% -> 2% of each run, Pallas kernels for 0% -> 0%
where the time goes in v4:
time: 100 us; the launch traced here: 98.5 us
  blocking collectives  44.2 us (44%)
  starting transfers between devices  32.6 us (33%)
  Pallas kernels  12.2 us (12%)
  waiting for transfers between devices  7.04 us (7%)
  local copies, waits for them, and re-layouts  1.03 us (1%)
    all_gather x1, blocking collectives, body(): kv_whole = lax.all_gather(kv_mine, REGION, axis=0, tiled=True)  27.5 us
    all_gather x1, blocking collectives, body(): parts = lax.all_gather(hop_part, 'third', axis=0, tiled=False)  16.6 us
    all_to_all x1, starting transfers between devices, body(): lax.all_to_all(sent, members, split_axis=0, concat_axis=0, tiled=True)  14.7 us
    all_to_all x1, starting transfers between devices, body(): lax.all_to_all(dq, members, split_axis=0, concat_axis=0, tiled=True)  10.9 us
    pallas_call x1, Pallas kernels, attention_call(): pl.pallas_call(attention_kernel, out_shape=(jax.ShapeDtypeStruct((blocks,...  8.13 us
    ppermute x1, waiting for transfers between devices, body(): piece = lax.ppermute(chip_part[lines // 2:].astype(BF16), 'hop', swap)  3.34 us
    pallas_call x1, Pallas kernels, pack_call(): pl.pallas_call(pack_kernel, grid=(PACK_STEPS,), out_shape=jax.ShapeDtypeS...  3.02 us
    all_to_all x1, waiting for transfers between devices, body(): lax.all_to_all(sent, members, split_axis=0, concat_axis=0, tiled=True)  2.76 us
  transfers between devices with their start and end apart: 5, of which 3 were waited for; matrix products, arithmetic and copies ran while one was open for 2% of the time, Pallas kernels for 0%

profile of v4, /device:TPU:1, one launch (start us, length us, event | category | flops | bytes accessed | tf_op | source)
XLA Modules:
  0.0 98.5 jit_solution(197799307963004916)
XLA Ops:
  0.6 0.0 copy-start
  0.6 3.0 %pack.1 = bf16[64,72,128]{2,1,0:T(8,128)(2,1)} custom-call(bf16[128,2048]{1,0:T(8,128)(2,1)} %q_ref.1, bf16[128,2048]{1,0:T(8,128)(2,1)} %g_ref.1, bf16[128,2048]{1,0:T(8,128)(2,1)} %o_ref.1), custom_call_target="tpu_custom_call" | custom-call | tf_op jit(solution)/shard_map/pack/pallas_call | solution.py:206
  3.7 0.0 copy-start.1
  3.7 0.0 copy-start.2
  3.7 14.7 %all-to-all-start = ((bf16[64,72,128]{2,1,0:T(8,128)(2,1)}), bf16[64,72,128]{2,1,0:T(8,128)(2,1)S(1)}, u32[]{:S(2)}, u32[]{:S(2)}) async-start(bf16[64,72,128]{2,1,0:T(8,128)(2,1)} %pack.1), calls=%async_computation | async-start | bytes 2359296 | tf_op jit(solution)/shard_map/all_to_all | solution.py:254
  18.4 0.1 pad_add_fusion.place_ref
  18.5 0.0 copy-done
  18.5 27.5 %all_gather.9 = bf16[1536,128]{1,0:T(8,128)(2,1)S(1)} all-gather(bf16[128,128]{1,0:T(8,128)(2,1)S(1)} %constant_dynamic-slice_fusion), channel_id=1, replica_groups=mesh['third'=3,'hop'=2,'step'=2,'chip'=32,'core'=2] {'third','hop','step'}, dimensions={0}, use_global_device_ids=true | all-gather | bytes 425984 | tf_op jit(solution)/shard_map/all_gather | solution.py:257
  46.1 1.0 constant_dynamic-slice_fusion.1
  47.0 2.8 %all-to-all-done.x_ref = bf16[64,72,128]{2,1,0:T(8,128)(2,1)S(1)} async-done(((bf16[64,72,128]{2,1,0:T(8,128)(2,1)}), bf16[64,72,128]{2,1,0:T(8,128)(2,1)S(1)}, u32[]{:S(2)}, u32[]{:S(2)}) %all-to-all-start) | async-done | bytes 1179680 | tf_op jit(solution)/shard_map/all_to_all | solution.py:254
  49.8 0.0 copy-done.1
  49.8 0.0 copy-done.2
  49.8 8.1 %attention.1 = (bf16[64,32,128]{2,1,0:T(8,128)(2,1)}, f32[12,64,128]{2,1,0:T(8,128)S(1)}, bf16[12,64,128]{2,1,0:T(8,128)(2,1)S(1)}) custom-call(s32[8,128]{1,0:T(8,128)S(1)} %bitcast.9, s32[128]{0:T(128)S(1)} %copy-done.2, s32[2]{0:T(128)S(1)} %pad_add_fusion.place_ref, bf16[64,72,128]{2,1,0:T(8,128)(2,1)S(1)} %all-to-all-done.x_ref, f32[64,128]{1,0:T(8,128)S(1)} %bitcast.8, ...), custom_call_target="tpu_custom_call" | custom-call | tf_op jit(solution)/shard_map/attention/pallas_call | solution.py:223
  57.9 1.9 %collective-permute-start = (bf16[12,64,128]{2,1,0:T(8,128)(2,1)S(1)}, bf16[12,64,128]{2,1,0:T(8,128)(2,1)S(1)}, u32[]{:S(2)}, u32[]{:S(2)}) collective-permute-start(bf16[12,64,128]{2,1,0:T(8,128)(2,1)S(1)} %get-tuple-element.7), channel_id=1, source_target_pairs={{0,64},{64,0},{1,65},{65,1},{2,66},{66,2},{3,67},{67,3},{4,68},{68... | collective-permute-start | bytes 589832 | tf_op jit(solution)/shard_map/ppermute | solution.py:270
  59.9 10.9 %all-to-all-start.1 = ((bf16[64,32,128]{2,1,0:T(8,128)(2,1)}), bf16[64,32,128]{2,1,0:T(8,128)(2,1)S(1)}, u32[]{:S(2)}, u32[]{:S(2)}) async-start(bf16[64,32,128]{2,1,0:T(8,128)(2,1)} %get-tuple-element.5), calls=%async_computation.1 | async-start | bytes 1048576 | tf_op jit(solution)/shard_map/all_to_all | solution.py:268
  70.8 0.0 collective-permute-done
  70.8 0.1 convert_add_fusion
  70.8 2.4 %collective-permute-start.1 = (bf16[6,64,128]{2,1,0:T(8,128)(2,1)S(1)}, bf16[6,64,128]{2,1,0:T(8,128)(2,1)S(1)}, u32[]{:S(2)}, u32[]{:S(2)}) collective-permute-start(bf16[6,64,128]{2,1,0:T(8,128)(2,1)S(1)} %slice.28), channel_id=1, source_target_pairs={{0,1},{1,0},{2,3},{3,2},{4,5},{5,4},{6,7},{7,6},{8,9},{9,8},{10,11... | collective-permute-start | bytes 294920 | tf_op jit(solution)/shard_map/ppermute | solution.py:273
  73.2 0.9 collective-permute-done.1
  74.2 2.7 %collective-permute-start.2 = (bf16[3,64,128]{2,1,0:T(8,128)(2,1)S(1)}, bf16[3,64,128]{2,1,0:T(8,128)(2,1)S(1)}, u32[]{:S(2)}, u32[]{:S(2)}) collective-permute-start(bf16[3,64,128]{2,1,0:T(8,128)(2,1)S(1)} %slice.29), channel_id=1, source_target_pairs={{0,128},{128,0},{1,129},{129,1},{2,130},{130,2},{3,131},{131,3},{4... | collective-permute-start | bytes 147464 | tf_op jit(solution)/shard_map/ppermute | solution.py:275
  76.9 3.3 %collective-permute-done.2 = bf16[3,64,128]{2,1,0:T(8,128)(2,1)S(1)} collective-permute-done((bf16[3,64,128]{2,1,0:T(8,128)(2,1)S(1)}, bf16[3,64,128]{2,1,0:T(8,128)(2,1)S(1)}, u32[]{:S(2)}, u32[]{:S(2)}) %collective-permute-start.2) | collective-permute-done | bytes 49184 | tf_op jit(solution)/shard_map/ppermute | solution.py:275
  80.2 16.6 %all-gather = bf16[9,64,128]{2,1,0:T(8,128)(2,1)S(1)} all-gather(bf16[3,64,128]{2,1,0:T(8,128)(2,1)S(1)} %fusion), channel_id=2, replica_groups=mesh['third'=3,'hop'=2,'step'=2,'chip'=32,'core'=2] {'third'}, dimensions={0}, use_global_device_ids=true | all-gather | bytes 196608 | tf_op jit(solution)/shard_map/all_gather | solution.py:277
  96.9 0.6 convert_reduce_fusion
  97.5 0.0 all-to-all-done.1.y_ref
  97.5 1.0 %unpack.1 = bf16[128,2048]{1,0:T(8,128)(2,1)} custom-call(bf16[64,32,128]{2,1,0:T(8,128)(2,1)S(1)} %all-to-all-done.1.y_ref), custom_call_target="tpu_custom_call" | custom-call | tf_op jit(solution)/shard_map/unpack/pallas_call | solution.py:280
  (5 shorter events, 0.1 us)
Async XLA Ops:
  0.6 17.9 %copy-start = (bf16[128,4096]{1,0:T(8,128)(2,1)S(1)}, bf16[128,4096]{1,0:T(8,128)(2,1)}, u32[]{:S(2)}) copy-start(bf16[128,4096]{1,0:T(8,128)(2,1)} %param.11) | copy-start | bytes 3145732
  3.7 46.1 %copy-start.1 = (s32[128,8]{0,1:T(8,128)S(1)}, s32[128,8]{0,1:T(8,128)}, u32[]{:S(2)}) copy-start(s32[128,8]{0,1:T(8,128)} %param.12) | copy-start | bytes 12292
  3.7 46.1 %copy-start.2 = (s32[128]{0:T(128)S(1)}, s32[128]{0:T(128)}, u32[]{:S(2)}) copy-start(s32[128]{0:T(128)} %counts_ref.1) | copy-start | bytes 1540
  3.7 46.1 %all-to-all-start = ((bf16[64,72,128]{2,1,0:T(8,128)(2,1)}), bf16[64,72,128]{2,1,0:T(8,128)(2,1)S(1)}, u32[]{:S(2)}, u32[]{:S(2)}) async-start(bf16[64,72,128]{2,1,0:T(8,128)(2,1)} %pack.1), calls=%async_computation | async-start | bytes 2359296 | tf_op jit(solution)/shard_map/all_to_all | solution.py:254
  57.9 12.8 %collective-permute-start = (bf16[12,64,128]{2,1,0:T(8,128)(2,1)S(1)}, bf16[12,64,128]{2,1,0:T(8,128)(2,1)S(1)}, u32[]{:S(2)}, u32[]{:S(2)}) collective-permute-start(bf16[12,64,128]{2,1,0:T(8,128)(2,1)S(1)} %get-tuple-element.7), channel_id=1, source_target_pairs={{0,64},{64,0},{1,65},{65,1},{2,66},{66,2},{3,67},{67,3},{4,68},{68... | collective-permute-start | bytes 589832 | tf_op jit(solution)/shard_map/ppermute | solution.py:270
  59.9 37.6 %all-to-all-start.1 = ((bf16[64,32,128]{2,1,0:T(8,128)(2,1)}), bf16[64,32,128]{2,1,0:T(8,128)(2,1)S(1)}, u32[]{:S(2)}, u32[]{:S(2)}) async-start(bf16[64,32,128]{2,1,0:T(8,128)(2,1)} %get-tuple-element.5), calls=%async_computation.1 | async-start | bytes 1048576 | tf_op jit(solution)/shard_map/all_to_all | solution.py:268
  70.8 3.3 %collective-permute-start.1 = (bf16[6,64,128]{2,1,0:T(8,128)(2,1)S(1)}, bf16[6,64,128]{2,1,0:T(8,128)(2,1)S(1)}, u32[]{:S(2)}, u32[]{:S(2)}) collective-permute-start(bf16[6,64,128]{2,1,0:T(8,128)(2,1)S(1)} %slice.28), channel_id=1, source_target_pairs={{0,1},{1,0},{2,3},{3,2},{4,5},{5,4},{6,7},{7,6},{8,9},{9,8},{10,11... | collective-permute-start | bytes 294920 | tf_op jit(solution)/shard_map/ppermute | solution.py:273
  74.2 6.0 %collective-permute-start.2 = (bf16[3,64,128]{2,1,0:T(8,128)(2,1)S(1)}, bf16[3,64,128]{2,1,0:T(8,128)(2,1)S(1)}, u32[]{:S(2)}, u32[]{:S(2)}) collective-permute-start(bf16[3,64,128]{2,1,0:T(8,128)(2,1)S(1)} %slice.29), channel_id=1, source_target_pairs={{0,128},{128,0},{1,129},{129,1},{2,130},{130,2},{3,131},{131,3},{4... | collective-permute-start | bytes 147464 | tf_op jit(solution)/shard_map/ppermute | solution.py:275

commit v5 on v4

--- a/solution.py
+++ b/solution.py
@@ -63,10 +63,6 @@
             x_ref[2 * head + share, BLOCK : BLOCK + TAIL, :] = row.astype(BF16)
 
 
-def slot_of(line, my_region):
-    return (lax.rem(line, 2) ^ lax.rem(my_region // 2, 2)) * 3 + line // 2
-
-
 def attention_kernel(
     ids_ref,
     counts_ref,
@@ -76,7 +72,9 @@
     kv_ref,
     dq_ref,
     kept_ref,
-    given_ref,
+    one_ref,
+    two_ref,
+    three_ref,
     acc_ref,
     query_ref,
     later_ref,
@@ -162,23 +160,18 @@
 
     lax.fori_loop(0, (later + LATER_UNROLL - 1) // LATER_UNROLL, second_turn, 0)
 
-    def finish_kv(line, carry):
-        slot = slot_of(line, my_region)
-        lines = acc_ref.shape[0] // 4
-        for other in range(2):
-            region = 2 * line + (lax.rem(my_region, 2) ^ other)
+    def finish_kv(third, carry):
+        thirds = acc_ref.shape[0] // 8
+        for gap, part_ref in enumerate((kept_ref, one_ref, two_ref, three_ref)):
+            region = 4 * third + (lax.rem(my_region, 4) ^ gap)
             joined = jnp.concatenate([acc_ref[2 * region], acc_ref[2 * region + 1]], axis=0).T
             own_half = jnp.where(share == 0, joined[:HD], joined[HD:])
             other_half = jnp.where(share == 0, joined[HD:], joined[:HD])
-            if other == 0:
-                kept_ref[slot] = own_half
-                kept_ref[lines + slot] = other_half
-            else:
-                given_ref[slot] = own_half.astype(BF16)
-                given_ref[lines + slot] = other_half.astype(BF16)
-        return carry
-
-    lax.fori_loop(0, acc_ref.shape[0] // 4, finish_kv, 0, unroll=2)
+            part_ref[third] = own_half.astype(part_ref.dtype)
+            part_ref[thirds + third] = other_half.astype(part_ref.dtype)
+        return carry
+
+    lax.fori_loop(0, acc_ref.shape[0] // 8, finish_kv, 0)
 
 
 def unpack_kernel(y_ref, out_ref):
@@ -224,11 +217,11 @@
         attention_kernel,
         out_shape=(
             jax.ShapeDtypeStruct((blocks, BLOCK // 2, 128), BF16),
-            jax.ShapeDtypeStruct((global_blocks // 2, HD, 128), F32),
-            jax.ShapeDtypeStruct((global_blocks // 2, HD, 128), BF16),
+            jax.ShapeDtypeStruct((global_blocks // 4, HD, 128), F32),
+            *[jax.ShapeDtypeStruct((global_blocks // 4, HD, 128), BF16)] * 3,
         ),
         in_specs=[smem] * 3 + vmem(3),
-        out_specs=tuple(vmem(3)),
+        out_specs=tuple(vmem(5)),
         scratch_shapes=[
             pltpu.VMEM((global_blocks, BLOCK, 128), F32),
             pltpu.VMEM((blocks, BLOCK, 128), F32),
@@ -257,7 +250,7 @@
     kv_whole = lax.all_gather(kv_mine, REGION, axis=0, tiled=True)
     kv_blocks = kv_whole.reshape(-1, BLOCK, 2 * HD)
     norm_mine = lax.dynamic_slice_in_dim(log_norm, my_head, 1, 0).reshape(blocks, 128)
-    dq, kept, given = attention_call(
+    dq, kept, *given = attention_call(
         block_ids.T,
         block_counts,
         jnp.stack([my_share, lax.axis_index(REGION)]).astype(jnp.int32),
@@ -266,14 +259,13 @@
         kv_blocks,
     )
     returned = lax.all_to_all(dq, members, split_axis=0, concat_axis=0, tiled=True)
-    swap = [(0, 1), (1, 0)]
-    piece = lax.ppermute(given, "step", swap)
-    step_part = kept + piece.astype(F32)
-    lines = regions // 2
-    piece = lax.ppermute(step_part[lines:].astype(BF16), "core", swap)
-    chip_part = step_part[:lines] + piece.astype(F32)
-    piece = lax.ppermute(chip_part[lines // 2 :].astype(BF16), "hop", swap)
-    hop_part = (chip_part[: lines // 2] + piece.astype(F32)).astype(BF16)
+    near_part = kept
+    for gap, piece in enumerate(given, start=1):
+        route = [(i, i ^ gap) for i in range(4)]
+        near_part = near_part + lax.ppermute(piece, ("hop", "step"), route).astype(F32)
+    thirds = regions // 4
+    piece = lax.ppermute(near_part[thirds:].astype(BF16), "core", [(0, 1), (1, 0)])
+    hop_part = (near_part[:thirds] + piece.astype(F32)).astype(BF16)
     parts = lax.all_gather(hop_part, "third", axis=0, tiled=False)
     mine = lax.dynamic_index_in_dim(parts, lax.axis_index("third"), axis=1, keepdims=False)
     kv_grad = jnp.sum(mine.astype(F32), axis=0)

time: 100 us -> 105 us (1.050)
  starting transfers between devices: 32.6 us -> 37.5 us
  waiting for transfers between devices: 7.04 us -> 8.68 us
    ppermute x3 -> x4, starting transfers between devices: 6.95 us -> 11.9 us  [the longest x3 9.27 us: body(): lax.ppermute(piece, ('hop', 'step'), route).astype(F32)]
    ppermute x3 -> x4, waiting for transfers between devices: 4.27 us -> 5.91 us  [the longest x3 5.05 us: body(): lax.ppermute(piece, ('hop', 'step'), route).astype(F32)]
  transfers between devices with their start and end apart: 5 -> 6, of which waited for: 3 -> 4; matrix products, arithmetic and copies ran while one was open for 2% -> 2% of each run, Pallas kernels for 0% -> 0%
where the time goes in v5:
time: 105 us; the launch traced here: 104 us
  blocking collectives  43.3 us (41%)
  starting transfers between devices  37.5 us (36%)
  Pallas kernels  12.2 us (12%)
  waiting for transfers between devices  8.68 us (8%)
    all_gather x1, blocking collectives, body(): kv_whole = lax.all_gather(kv_mine, REGION, axis=0, tiled=True)  27.5 us
    all_gather x1, blocking collectives, body(): parts = lax.all_gather(hop_part, 'third', axis=0, tiled=False)  15.8 us
    all_to_all x1, starting transfers between devices, body(): lax.all_to_all(sent, members, split_axis=0, concat_axis=0, tiled=True)  14.7 us
    all_to_all x1, starting transfers between devices, body(): lax.all_to_all(dq, members, split_axis=0, concat_axis=0, tiled=True)  10.9 us
    ppermute x3, starting transfers between devices, body(): lax.ppermute(piece, ('hop', 'step'), route).astype(F32)  9.27 us
    pallas_call x1, Pallas kernels, attention_call(): pl.pallas_call(attention_kernel, out_shape=(jax.ShapeDtypeStruct((blocks,...  8.13 us
    ppermute x3, waiting for transfers between devices, body(): lax.ppermute(piece, ('hop', 'step'), route).astype(F32)  5.05 us
    pallas_call x1, Pallas kernels, pack_call(): pl.pallas_call(pack_kernel, grid=(PACK_STEPS,), out_shape=jax.ShapeDtypeS...  3.02 us
  transfers between devices with their start and end apart: 6, of which 4 were waited for; matrix products, arithmetic and copies ran while one was open for 2% of the time, Pallas kernels for 0%

profile of v5, /device:TPU:1, one launch (start us, length us, event | category | flops | bytes accessed | tf_op | source)
XLA Modules:
  0.0 104.2 jit_solution(1055506040317199098)
XLA Ops:
  0.6 0.0 copy-start
  0.6 3.0 %pack.1 = bf16[64,72,128]{2,1,0:T(8,128)(2,1)} custom-call(bf16[128,2048]{1,0:T(8,128)(2,1)} %q_ref.1, bf16[128,2048]{1,0:T(8,128)(2,1)} %g_ref.1, bf16[128,2048]{1,0:T(8,128)(2,1)} %o_ref.1), custom_call_target="tpu_custom_call" | custom-call | tf_op jit(solution)/shard_map/pack/pallas_call | solution.py:199
  3.7 0.0 copy-start.1
  3.7 0.0 copy-start.2
  3.7 14.7 %all-to-all-start = ((bf16[64,72,128]{2,1,0:T(8,128)(2,1)}), bf16[64,72,128]{2,1,0:T(8,128)(2,1)S(1)}, u32[]{:S(2)}, u32[]{:S(2)}) async-start(bf16[64,72,128]{2,1,0:T(8,128)(2,1)} %pack.1), calls=%async_computation | async-start | bytes 2359296 | tf_op jit(solution)/shard_map/all_to_all | solution.py:247
  18.4 0.1 pad_add_fusion.place_ref
  18.5 0.0 copy-done
  18.5 27.5 %all_gather.9 = bf16[1536,128]{1,0:T(8,128)(2,1)S(1)} all-gather(bf16[128,128]{1,0:T(8,128)(2,1)S(1)} %constant_dynamic-slice_fusion), channel_id=1, replica_groups=mesh['third'=3,'hop'=2,'step'=2,'chip'=32,'core'=2] {'third','hop','step'}, dimensions={0}, use_global_device_ids=true | all-gather | bytes 425984 | tf_op jit(solution)/shard_map/all_gather | solution.py:250
  46.1 1.0 constant_dynamic-slice_fusion.1
  47.0 2.8 %all-to-all-done.x_ref = bf16[64,72,128]{2,1,0:T(8,128)(2,1)S(1)} async-done(((bf16[64,72,128]{2,1,0:T(8,128)(2,1)}), bf16[64,72,128]{2,1,0:T(8,128)(2,1)S(1)}, u32[]{:S(2)}, u32[]{:S(2)}) %all-to-all-start) | async-done | bytes 1179680 | tf_op jit(solution)/shard_map/all_to_all | solution.py:247
  49.8 0.0 copy-done.1
  49.8 0.0 copy-done.2
  49.8 8.1 %attention.1 = (bf16[64,32,128]{2,1,0:T(8,128)(2,1)}, f32[6,64,128]{2,1,0:T(8,128)S(1)}, bf16[6,64,128]{2,1,0:T(8,128)(2,1)S(1)}, bf16[6,64,128]{2,1,0:T(8,128)(2,1)S(1)}, bf16[6,64,128]{2,1,0:T(8,128)(2,1)S(1)}) custom-call(s32[8,128]{1,0:T(8,128)S(1)} %bitcast.9, s32[128]{0:T(128)S(1)} %copy-done.2, s32[2]{0:T(128)S(1)} %pad_add_fusion.place_ref, ...), custom_call_target="tpu_custom_call" | custom-call | tf_op jit(solution)/shard_map/attention/pallas_call | solution.py:216
  57.9 10.9 %all-to-all-start.1 = ((bf16[64,32,128]{2,1,0:T(8,128)(2,1)}), bf16[64,32,128]{2,1,0:T(8,128)(2,1)S(1)}, u32[]{:S(2)}, u32[]{:S(2)}) async-start(bf16[64,32,128]{2,1,0:T(8,128)(2,1)} %get-tuple-element.7), calls=%async_computation.1 | async-start | bytes 1048576 | tf_op jit(solution)/shard_map/all_to_all | solution.py:261
  68.8 1.9 %collective-permute-start.2 = (bf16[6,64,128]{2,1,0:T(8,128)(2,1)S(1)}, bf16[6,64,128]{2,1,0:T(8,128)(2,1)S(1)}, u32[]{:S(2)}, u32[]{:S(2)}) collective-permute-start(bf16[6,64,128]{2,1,0:T(8,128)(2,1)S(1)} %get-tuple-element.11), channel_id=1, source_target_pairs={{0,192},{64,128},{128,64},{192,0},{1,193},{65,129},{129,65},{193,1... | collective-permute-start | bytes 294920 | tf_op jit(solution)/shard_map/ppermute | solution.py:265
  70.8 2.7 %collective-permute-start.1 = (bf16[6,64,128]{2,1,0:T(8,128)(2,1)S(1)}, bf16[6,64,128]{2,1,0:T(8,128)(2,1)S(1)}, u32[]{:S(2)}, u32[]{:S(2)}) collective-permute-start(bf16[6,64,128]{2,1,0:T(8,128)(2,1)S(1)} %get-tuple-element.10), channel_id=1, source_target_pairs={{0,128},{64,192},{128,0},{192,64},{1,129},{65,193},{129,1},{193,65... | collective-permute-start | bytes 294920 | tf_op jit(solution)/shard_map/ppermute | solution.py:265
  73.5 4.7 %collective-permute-start = (bf16[6,64,128]{2,1,0:T(8,128)(2,1)S(1)}, bf16[6,64,128]{2,1,0:T(8,128)(2,1)S(1)}, u32[]{:S(2)}, u32[]{:S(2)}) collective-permute-start(bf16[6,64,128]{2,1,0:T(8,128)(2,1)S(1)} %get-tuple-element.9), channel_id=1, source_target_pairs={{0,64},{64,0},{128,192},{192,128},{1,65},{65,1},{129,193},{193,129... | collective-permute-start | bytes 294920 | tf_op jit(solution)/shard_map/ppermute | solution.py:265
  78.1 0.0 collective-permute-done.2
  78.1 3.4 %collective-permute-done.1 = bf16[6,64,128]{2,1,0:T(8,128)(2,1)S(1)} collective-permute-done((bf16[6,64,128]{2,1,0:T(8,128)(2,1)S(1)}, bf16[6,64,128]{2,1,0:T(8,128)(2,1)S(1)}, u32[]{:S(2)}, u32[]{:S(2)}) %collective-permute-start.1) | collective-permute-done | bytes 98336 | tf_op jit(solution)/shard_map/ppermute | solution.py:265
  81.5 1.7 %collective-permute-done = bf16[6,64,128]{2,1,0:T(8,128)(2,1)S(1)} collective-permute-done((bf16[6,64,128]{2,1,0:T(8,128)(2,1)S(1)}, bf16[6,64,128]{2,1,0:T(8,128)(2,1)S(1)}, u32[]{:S(2)}, u32[]{:S(2)}) %collective-permute-start) | collective-permute-done | bytes 98336 | tf_op jit(solution)/shard_map/ppermute | solution.py:265
  83.2 0.1 convert_add_fusion
  83.3 2.6 %collective-permute-start.3 = (bf16[3,64,128]{2,1,0:T(8,128)(2,1)S(1)}, bf16[3,64,128]{2,1,0:T(8,128)(2,1)S(1)}, u32[]{:S(2)}, u32[]{:S(2)}) collective-permute-start(bf16[3,64,128]{2,1,0:T(8,128)(2,1)S(1)} %slice.15), channel_id=1, source_target_pairs={{0,1},{1,0},{2,3},{3,2},{4,5},{5,4},{6,7},{7,6},{8,9},{9,8},{10,11... | collective-permute-start | bytes 147464 | tf_op jit(solution)/shard_map/ppermute | solution.py:267
  85.9 0.9 collective-permute-done.3
  86.7 15.8 %all-gather = bf16[9,64,128]{2,1,0:T(8,128)(2,1)S(1)} all-gather(bf16[3,64,128]{2,1,0:T(8,128)(2,1)S(1)} %fusion), channel_id=2, replica_groups=mesh['third'=3,'hop'=2,'step'=2,'chip'=32,'core'=2] {'third'}, dimensions={0}, use_global_device_ids=true | all-gather | bytes 196608 | tf_op jit(solution)/shard_map/all_gather | solution.py:269
  102.5 0.6 convert_reduce_fusion
  103.1 0.0 all-to-all-done.1.y_ref
  103.1 1.0 unpack.1
  (3 shorter events, 0.0 us)
Async XLA Ops:
  0.6 17.9 %copy-start = (bf16[128,4096]{1,0:T(8,128)(2,1)S(1)}, bf16[128,4096]{1,0:T(8,128)(2,1)}, u32[]{:S(2)}) copy-start(bf16[128,4096]{1,0:T(8,128)(2,1)} %param.11) | copy-start | bytes 3145732
  3.7 46.1 %copy-start.1 = (s32[128,8]{0,1:T(8,128)S(1)}, s32[128,8]{0,1:T(8,128)}, u32[]{:S(2)}) copy-start(s32[128,8]{0,1:T(8,128)} %param.12) | copy-start | bytes 12292
  3.7 46.1 %copy-start.2 = (s32[128]{0:T(128)S(1)}, s32[128]{0:T(128)}, u32[]{:S(2)}) copy-start(s32[128]{0:T(128)} %counts_ref.1) | copy-start | bytes 1540
  3.7 46.1 %all-to-all-start = ((bf16[64,72,128]{2,1,0:T(8,128)(2,1)}), bf16[64,72,128]{2,1,0:T(8,128)(2,1)S(1)}, u32[]{:S(2)}, u32[]{:S(2)}) async-start(bf16[64,72,128]{2,1,0:T(8,128)(2,1)} %pack.1), calls=%async_computation | async-start | bytes 2359296 | tf_op jit(solution)/shard_map/all_to_all | solution.py:247
  57.9 45.2 %all-to-all-start.1 = ((bf16[64,32,128]{2,1,0:T(8,128)(2,1)}), bf16[64,32,128]{2,1,0:T(8,128)(2,1)S(1)}, u32[]{:S(2)}, u32[]{:S(2)}) async-start(bf16[64,32,128]{2,1,0:T(8,128)(2,1)} %get-tuple-element.7), calls=%async_computation.1 | async-start | bytes 1048576 | tf_op jit(solution)/shard_map/all_to_all | solution.py:261
  68.8 9.3 %collective-permute-start.2 = (bf16[6,64,128]{2,1,0:T(8,128)(2,1)S(1)}, bf16[6,64,128]{2,1,0:T(8,128)(2,1)S(1)}, u32[]{:S(2)}, u32[]{:S(2)}) collective-permute-start(bf16[6,64,128]{2,1,0:T(8,128)(2,1)S(1)} %get-tuple-element.11), channel_id=1, source_target_pairs={{0,192},{64,128},{128,64},{192,0},{1,193},{65,129},{129,65},{193,1... | collective-permute-start | bytes 294920 | tf_op jit(solution)/shard_map/ppermute | solution.py:265
  70.8 10.8 %collective-permute-start.1 = (bf16[6,64,128]{2,1,0:T(8,128)(2,1)S(1)}, bf16[6,64,128]{2,1,0:T(8,128)(2,1)S(1)}, u32[]{:S(2)}, u32[]{:S(2)}) collective-permute-start(bf16[6,64,128]{2,1,0:T(8,128)(2,1)S(1)} %get-tuple-element.10), channel_id=1, source_target_pairs={{0,128},{64,192},{128,0},{192,64},{1,129},{65,193},{129,1},{193,65... | collective-permute-start | bytes 294920 | tf_op jit(solution)/shard_map/ppermute | solution.py:265
  73.5 9.7 %collective-permute-start = (bf16[6,64,128]{2,1,0:T(8,128)(2,1)S(1)}, bf16[6,64,128]{2,1,0:T(8,128)(2,1)S(1)}, u32[]{:S(2)}, u32[]{:S(2)}) collective-permute-start(bf16[6,64,128]{2,1,0:T(8,128)(2,1)S(1)} %get-tuple-element.9), channel_id=1, source_target_pairs={{0,64},{64,0},{128,192},{192,128},{1,65},{65,1},{129,193},{193,129... | collective-permute-start | bytes 294920 | tf_op jit(solution)/shard_map/ppermute | solution.py:265
  83.3 3.5 %collective-permute-start.3 = (bf16[3,64,128]{2,1,0:T(8,128)(2,1)S(1)}, bf16[3,64,128]{2,1,0:T(8,128)(2,1)S(1)}, u32[]{:S(2)}, u32[]{:S(2)}) collective-permute-start(bf16[3,64,128]{2,1,0:T(8,128)(2,1)S(1)} %slice.15), channel_id=1, source_target_pairs={{0,1},{1,0},{2,3},{3,2},{4,5},{5,4},{6,7},{7,6},{8,9},{9,8},{10,11... | collective-permute-start | bytes 147464 | tf_op jit(solution)/shard_map/ppermute | solution.py:267

commit v6 on v4

--- a/solution.py
+++ b/solution.py
@@ -10,7 +10,7 @@
 BLOCK = 64
 SCALE = 0.125
 GROUP = 4
-UNROLL = 32
+UNROLL = 64
 LATER_UNROLL = 8
 PACK_STEPS = 2
 TAIL = 8
@@ -64,7 +64,8 @@
 
 
 def slot_of(line, my_region):
-    return (lax.rem(line, 2) ^ lax.rem(my_region // 2, 2)) * 3 + line // 2
+    ahead = lax.rem(line // 2 - my_region // 4 + 3, 3)
+    return (lax.rem(line, 2) ^ lax.rem(my_region // 2, 2)) * 3 + ahead
 
 
 def attention_kernel(
@@ -273,10 +274,11 @@
     piece = lax.ppermute(step_part[lines:].astype(BF16), "core", swap)
     chip_part = step_part[:lines] + piece.astype(F32)
     piece = lax.ppermute(chip_part[lines // 2 :].astype(BF16), "hop", swap)
-    hop_part = (chip_part[: lines // 2] + piece.astype(F32)).astype(BF16)
-    parts = lax.all_gather(hop_part, "third", axis=0, tiled=False)
-    mine = lax.dynamic_index_in_dim(parts, lax.axis_index("third"), axis=1, keepdims=False)
-    kv_grad = jnp.sum(mine.astype(F32), axis=0)
+    hop_part = chip_part[: lines // 2] + piece.astype(F32)
+    far = []
+    for k in (1, 2):
+        route = [(i, (i + k) % 3) for i in range(3)]
+        far.append(lax.ppermute(hop_part[k].astype(BF16), "third", route))
     query_grad = pl.pallas_call(
         unpack_kernel,
         out_shape=jax.ShapeDtypeStruct(query.shape, BF16),
@@ -285,6 +287,10 @@
         compiler_params=limit,
         name="unpack",
     )(returned)
+    query_grad, *far = lax.optimization_barrier((query_grad, *far))
+    kv_grad = hop_part[0]
+    for piece in far:
+        kv_grad = kv_grad + piece.astype(F32)
     return (query_grad, kv_grad.T)
 
 

time: 100 us -> 97.3 us (0.973)
  blocking collectives: 44.2 us -> 27.5 us
  starting transfers between devices: 32.6 us -> 44.7 us
  waiting for transfers between devices: 7.04 us -> 10.6 us
  Pallas kernels: 12.2 us -> 11 us
    all_gather x1 -> x0, blocking collectives: 16.6 us -> none  [body(): parts = lax.all_gather(hop_part, 'third', axis=0, tiled=False)]
    ppermute x0 -> x2, starting transfers between devices: none -> 10.5 us  [body(): far.append(lax.ppermute(hop_part[k].astype(BF16), 'third', route))]
    ppermute x0 -> x2, waiting for transfers between devices: none -> 3.61 us  [body(): far.append(lax.ppermute(hop_part[k].astype(BF16), 'third', route))]
    all_to_all x1, starting transfers between devices: 10.9 us -> 12.5 us  [body(): lax.all_to_all(dq, members, split_axis=0, concat_axis=0, tiled=True)]
    pallas_call x1, Pallas kernels: 8.13 us -> 6.95 us  [attention_call(): pl.pallas_call(attention_kernel, out_shape=(jax.ShapeDtypeStruct((blocks,...]
  transfers between devices with their start and end apart: 5 -> 7, of which waited for: 3 -> 4; matrix products, arithmetic and copies ran while one was open for 2% -> 1% of each run, Pallas kernels for 0% -> 1%
where the time goes in v6:
time: 97.3 us; the launch traced here: 96.4 us
  starting transfers between devices  44.7 us (46%)
  blocking collectives  27.5 us (28%)
  Pallas kernels  11 us (11%)
  waiting for transfers between devices  10.6 us (11%)
  local copies, waits for them, and re-layouts  1.03 us (1%)
    all_gather x1, blocking collectives, body(): kv_whole = lax.all_gather(kv_mine, REGION, axis=0, tiled=True)  27.5 us
    all_to_all x1, starting transfers between devices, body(): lax.all_to_all(sent, members, split_axis=0, concat_axis=0, tiled=True)  14.7 us
    all_to_all x1, starting transfers between devices, body(): lax.all_to_all(dq, members, split_axis=0, concat_axis=0, tiled=True)  12.5 us
    ppermute x2, starting transfers between devices, body(): far.append(lax.ppermute(hop_part[k].astype(BF16), 'third', route))  10.5 us
    pallas_call x1, Pallas kernels, attention_call(): pl.pallas_call(attention_kernel, out_shape=(jax.ShapeDtypeStruct((blocks,...  6.95 us
    ppermute x2, waiting for transfers between devices, body(): far.append(lax.ppermute(hop_part[k].astype(BF16), 'third', route))  3.61 us
    ppermute x1, waiting for transfers between devices, body(): piece = lax.ppermute(chip_part[lines // 2:].astype(BF16), 'hop', swap)  3.34 us
    pallas_call x1, Pallas kernels, pack_call(): pl.pallas_call(pack_kernel, grid=(PACK_STEPS,), out_shape=jax.ShapeDtypeS...  3.02 us
  transfers between devices with their start and end apart: 7, of which 4 were waited for; matrix products, arithmetic and copies ran while one was open for 1% of the time, Pallas kernels for 1%

profile of v6, /device:TPU:1, one launch (start us, length us, event | category | flops | bytes accessed | tf_op | source)
XLA Modules:
  0.0 96.4 jit_solution(13746395553278796355)
XLA Ops:
  0.6 0.0 copy-start
  0.6 3.0 %pack.1 = bf16[64,72,128]{2,1,0:T(8,128)(2,1)} custom-call(bf16[128,2048]{1,0:T(8,128)(2,1)} %q_ref.1, bf16[128,2048]{1,0:T(8,128)(2,1)} %g_ref.1, bf16[128,2048]{1,0:T(8,128)(2,1)} %o_ref.1), custom_call_target="tpu_custom_call" | custom-call | tf_op jit(solution)/shard_map/pack/pallas_call | solution.py:207
  3.7 0.0 copy-start.1
  3.7 0.0 copy-start.2
  3.7 14.7 %all-to-all-start = ((bf16[64,72,128]{2,1,0:T(8,128)(2,1)}), bf16[64,72,128]{2,1,0:T(8,128)(2,1)S(1)}, u32[]{:S(2)}, u32[]{:S(2)}) async-start(bf16[64,72,128]{2,1,0:T(8,128)(2,1)} %pack.1), calls=%async_computation | async-start | bytes 2359296 | tf_op jit(solution)/shard_map/all_to_all | solution.py:255
  18.4 0.1 pad_add_fusion.place_ref
  18.5 0.0 copy-done
  18.5 27.5 %all_gather.3 = bf16[1536,128]{1,0:T(8,128)(2,1)S(1)} all-gather(bf16[128,128]{1,0:T(8,128)(2,1)S(1)} %constant_dynamic-slice_fusion), channel_id=1, replica_groups=mesh['third'=3,'hop'=2,'step'=2,'chip'=32,'core'=2] {'third','hop','step'}, dimensions={0}, use_global_device_ids=true | all-gather | bytes 425984 | tf_op jit(solution)/shard_map/all_gather | solution.py:258
  46.1 1.0 %constant_dynamic-slice_fusion.1 = f32[1,8192]{1,0:T(1,128)S(1)} fusion(f32[32,8192]{1,0:T(8,128)} %param.10, s32[]{:T(128)S(6)} %select_n.6), kind=kLoop, calls=%fused_computation.13 | loop fusion | bytes 65540 | tf_op jit(solution)/shard_map/dynamic_slice | solution.py:260
  47.0 2.8 %all-to-all-done.x_ref = bf16[64,72,128]{2,1,0:T(8,128)(2,1)S(1)} async-done(((bf16[64,72,128]{2,1,0:T(8,128)(2,1)}), bf16[64,72,128]{2,1,0:T(8,128)(2,1)S(1)}, u32[]{:S(2)}, u32[]{:S(2)}) %all-to-all-start) | async-done | bytes 1179680 | tf_op jit(solution)/shard_map/all_to_all | solution.py:255
  49.8 0.0 copy-done.1
  49.8 0.0 copy-done.2
  49.8 6.9 %attention.1 = (bf16[64,32,128]{2,1,0:T(8,128)(2,1)}, f32[12,64,128]{2,1,0:T(8,128)S(1)}, bf16[12,64,128]{2,1,0:T(8,128)(2,1)S(1)}) custom-call(s32[8,128]{1,0:T(8,128)S(1)} %bitcast.21, s32[128]{0:T(128)S(1)} %copy-done.2, s32[2]{0:T(128)S(1)} %pad_add_fusion.place_ref, bf16[64,72,128]{2,1,0:T(8,128)(2,1)S(1)} %all-to-all-done.x_ref, ...), custom_call_target="tpu_custom_call" | custom-call | tf_op jit(solution)/shard_map/attention/pallas_call | solution.py:224
  56.8 1.9 %collective-permute-start = (bf16[12,64,128]{2,1,0:T(8,128)(2,1)S(1)}, bf16[12,64,128]{2,1,0:T(8,128)(2,1)S(1)}, u32[]{:S(2)}, u32[]{:S(2)}) collective-permute-start(bf16[12,64,128]{2,1,0:T(8,128)(2,1)S(1)} %get-tuple-element.10), channel_id=1, source_target_pairs={{0,64},{64,0},{1,65},{65,1},{2,66},{66,2},{3,67},{67,3},{4,68},{68... | collective-permute-start | bytes 589832 | tf_op jit(solution)/shard_map/ppermute | solution.py:271
  58.7 12.5 %all-to-all-start.1 = ((bf16[64,32,128]{2,1,0:T(8,128)(2,1)}), bf16[64,32,128]{2,1,0:T(8,128)(2,1)S(1)}, u32[]{:S(2)}, u32[]{:S(2)}) async-start(bf16[64,32,128]{2,1,0:T(8,128)(2,1)} %get-tuple-element.8), calls=%async_computation.1 | async-start | bytes 1048576 | tf_op jit(solution)/shard_map/all_to_all | solution.py:269
  71.2 0.0 collective-permute-done
  71.2 0.1 convert_add_fusion
  71.3 2.4 %collective-permute-start.1 = (bf16[6,64,128]{2,1,0:T(8,128)(2,1)S(1)}, bf16[6,64,128]{2,1,0:T(8,128)(2,1)S(1)}, u32[]{:S(2)}, u32[]{:S(2)}) collective-permute-start(bf16[6,64,128]{2,1,0:T(8,128)(2,1)S(1)} %slice.52), channel_id=1, source_target_pairs={{0,1},{1,0},{2,3},{3,2},{4,5},{5,4},{6,7},{7,6},{8,9},{9,8},{10,11... | collective-permute-start | bytes 294920 | tf_op jit(solution)/shard_map/ppermute | solution.py:274
  73.6 0.9 collective-permute-done.1
  74.6 2.7 %collective-permute-start.2 = (bf16[3,64,128]{2,1,0:T(8,128)(2,1)S(1)}, bf16[3,64,128]{2,1,0:T(8,128)(2,1)S(1)}, u32[]{:S(2)}, u32[]{:S(2)}) collective-permute-start(bf16[3,64,128]{2,1,0:T(8,128)(2,1)S(1)} %slice.53), channel_id=1, source_target_pairs={{0,128},{128,0},{1,129},{129,1},{2,130},{130,2},{3,131},{131,3},{4... | collective-permute-start | bytes 147464 | tf_op jit(solution)/shard_map/ppermute | solution.py:276
  77.3 3.3 %collective-permute-done.2 = bf16[3,64,128]{2,1,0:T(8,128)(2,1)S(1)} collective-permute-done((bf16[3,64,128]{2,1,0:T(8,128)(2,1)S(1)}, bf16[3,64,128]{2,1,0:T(8,128)(2,1)S(1)}, u32[]{:S(2)}, u32[]{:S(2)}) %collective-permute-start.2) | collective-permute-done | bytes 49184 | tf_op jit(solution)/shard_map/ppermute | solution.py:276
  80.7 6.7 %collective-permute-start.3 = (bf16[64,128]{1,0:T(8,128)(2,1)S(1)}, bf16[64,128]{1,0:T(8,128)(2,1)S(1)}, u32[]{:S(2)}, u32[]{:S(2)}) collective-permute-start(bf16[64,128]{1,0:T(8,128)(2,1)S(1)} %get-tuple-element.17), channel_id=1, source_target_pairs={{0,256},{256,512},{512,0},{1,257},{257,513},{513,1},{2,258},{258,5... | collective-permute-start | bytes 49160 | tf_op jit(solution)/shard_map/ppermute | solution.py:281
  87.4 3.7 %collective-permute-start.4 = (bf16[64,128]{1,0:T(8,128)(2,1)S(1)}, bf16[64,128]{1,0:T(8,128)(2,1)S(1)}, u32[]{:S(2)}, u32[]{:S(2)}) collective-permute-start(bf16[64,128]{1,0:T(8,128)(2,1)S(1)} %get-tuple-element.16), channel_id=1, source_target_pairs={{0,512},{256,0},{512,256},{1,513},{257,1},{513,257},{2,514},{258,2... | collective-permute-start | bytes 49160 | tf_op jit(solution)/shard_map/ppermute | solution.py:281
  91.1 0.0 all-to-all-done.1.y_ref
  91.2 1.0 %unpack.1 = bf16[128,2048]{1,0:T(8,128)(2,1)} custom-call(bf16[64,32,128]{2,1,0:T(8,128)(2,1)S(1)} %all-to-all-done.1.y_ref), custom_call_target="tpu_custom_call" | custom-call | tf_op jit(solution)/shard_map/unpack/pallas_call | solution.py:282
  92.2 0.0 collective-permute-done.3
  92.2 3.6 %collective-permute-done.4 = bf16[64,128]{1,0:T(8,128)(2,1)S(1)} collective-permute-done((bf16[64,128]{1,0:T(8,128)(2,1)S(1)}, bf16[64,128]{1,0:T(8,128)(2,1)S(1)}, u32[]{:S(2)}, u32[]{:S(2)}) %collective-permute-start.4) | collective-permute-done | bytes 16416 | tf_op jit(solution)/shard_map/ppermute | solution.py:281
  95.8 0.6 fusion.2
  (6 shorter events, 0.1 us)
Async XLA Ops:
  0.6 17.9 %copy-start = (bf16[128,4096]{1,0:T(8,128)(2,1)S(1)}, bf16[128,4096]{1,0:T(8,128)(2,1)}, u32[]{:S(2)}) copy-start(bf16[128,4096]{1,0:T(8,128)(2,1)} %param.11) | copy-start | bytes 3145732
  3.7 46.1 %copy-start.1 = (s32[128,8]{0,1:T(8,128)S(1)}, s32[128,8]{0,1:T(8,128)}, u32[]{:S(2)}) copy-start(s32[128,8]{0,1:T(8,128)} %param.12) | copy-start | bytes 12292
  3.7 46.1 %copy-start.2 = (s32[128]{0:T(128)S(1)}, s32[128]{0:T(128)}, u32[]{:S(2)}) copy-start(s32[128]{0:T(128)} %counts_ref.1) | copy-start | bytes 1540
  3.7 46.1 %all-to-all-start = ((bf16[64,72,128]{2,1,0:T(8,128)(2,1)}), bf16[64,72,128]{2,1,0:T(8,128)(2,1)S(1)}, u32[]{:S(2)}, u32[]{:S(2)}) async-start(bf16[64,72,128]{2,1,0:T(8,128)(2,1)} %pack.1), calls=%async_computation | async-start | bytes 2359296 | tf_op jit(solution)/shard_map/all_to_all | solution.py:255
  56.8 14.4 %collective-permute-start = (bf16[12,64,128]{2,1,0:T(8,128)(2,1)S(1)}, bf16[12,64,128]{2,1,0:T(8,128)(2,1)S(1)}, u32[]{:S(2)}, u32[]{:S(2)}) collective-permute-start(bf16[12,64,128]{2,1,0:T(8,128)(2,1)S(1)} %get-tuple-element.10), channel_id=1, source_target_pairs={{0,64},{64,0},{1,65},{65,1},{2,66},{66,2},{3,67},{67,3},{4,68},{68... | collective-permute-start | bytes 589832 | tf_op jit(solution)/shard_map/ppermute | solution.py:271
  58.7 32.5 %all-to-all-start.1 = ((bf16[64,32,128]{2,1,0:T(8,128)(2,1)}), bf16[64,32,128]{2,1,0:T(8,128)(2,1)S(1)}, u32[]{:S(2)}, u32[]{:S(2)}) async-start(bf16[64,32,128]{2,1,0:T(8,128)(2,1)} %get-tuple-element.8), calls=%async_computation.1 | async-start | bytes 1048576 | tf_op jit(solution)/shard_map/all_to_all | solution.py:269
  71.3 3.3 %collective-permute-start.1 = (bf16[6,64,128]{2,1,0:T(8,128)(2,1)S(1)}, bf16[6,64,128]{2,1,0:T(8,128)(2,1)S(1)}, u32[]{:S(2)}, u32[]{:S(2)}) collective-permute-start(bf16[6,64,128]{2,1,0:T(8,128)(2,1)S(1)} %slice.52), channel_id=1, source_target_pairs={{0,1},{1,0},{2,3},{3,2},{4,5},{5,4},{6,7},{7,6},{8,9},{9,8},{10,11... | collective-permute-start | bytes 294920 | tf_op jit(solution)/shard_map/ppermute | solution.py:274
  74.6 6.0 %collective-permute-start.2 = (bf16[3,64,128]{2,1,0:T(8,128)(2,1)S(1)}, bf16[3,64,128]{2,1,0:T(8,128)(2,1)S(1)}, u32[]{:S(2)}, u32[]{:S(2)}) collective-permute-start(bf16[3,64,128]{2,1,0:T(8,128)(2,1)S(1)} %slice.53), channel_id=1, source_target_pairs={{0,128},{128,0},{1,129},{129,1},{2,130},{130,2},{3,131},{131,3},{4... | collective-permute-start | bytes 147464 | tf_op jit(solution)/shard_map/ppermute | solution.py:276
  80.7 11.5 %collective-permute-start.3 = (bf16[64,128]{1,0:T(8,128)(2,1)S(1)}, bf16[64,128]{1,0:T(8,128)(2,1)S(1)}, u32[]{:S(2)}, u32[]{:S(2)}) collective-permute-start(bf16[64,128]{1,0:T(8,128)(2,1)S(1)} %get-tuple-element.17), channel_id=1, source_target_pairs={{0,256},{256,512},{512,0},{1,257},{257,513},{513,1},{2,258},{258,5... | collective-permute-start | bytes 49160 | tf_op jit(solution)/shard_map/ppermute | solution.py:281
  87.4 8.4 %collective-permute-start.4 = (bf16[64,128]{1,0:T(8,128)(2,1)S(1)}, bf16[64,128]{1,0:T(8,128)(2,1)S(1)}, u32[]{:S(2)}, u32[]{:S(2)}) collective-permute-start(bf16[64,128]{1,0:T(8,128)(2,1)S(1)} %get-tuple-element.16), channel_id=1, source_target_pairs={{0,512},{256,0},{512,256},{1,513},{257,1},{513,257},{2,514},{258,2... | collective-permute-start | bytes 49160 | tf_op jit(solution)/shard_map/ppermute | solution.py:281

commit v7 on v6

--- a/solution.py
+++ b/solution.py
@@ -65,7 +65,7 @@
 
 def slot_of(line, my_region):
     ahead = lax.rem(line // 2 - my_region // 4 + 3, 3)
-    return (lax.rem(line, 2) ^ lax.rem(my_region // 2, 2)) * 3 + ahead
+    return (lax.rem(line, 2) ^ lax.rem(my_region, 2)) * 3 + ahead
 
 
 def attention_kernel(
@@ -167,7 +167,8 @@
         slot = slot_of(line, my_region)
         lines = acc_ref.shape[0] // 4
         for other in range(2):
-            region = 2 * line + (lax.rem(my_region, 2) ^ other)
+            hop = lax.rem(my_region // 2, 2) ^ other
+            region = line // 2 * 4 + hop * 2 + lax.rem(line, 2)
             joined = jnp.concatenate([acc_ref[2 * region], acc_ref[2 * region + 1]], axis=0).T
             own_half = jnp.where(share == 0, joined[:HD], joined[HD:])
             other_half = jnp.where(share == 0, joined[HD:], joined[:HD])
@@ -268,12 +269,12 @@
     )
     returned = lax.all_to_all(dq, members, split_axis=0, concat_axis=0, tiled=True)
     swap = [(0, 1), (1, 0)]
-    piece = lax.ppermute(given, "step", swap)
+    piece = lax.ppermute(given, "hop", swap)
     step_part = kept + piece.astype(F32)
     lines = regions // 2
     piece = lax.ppermute(step_part[lines:].astype(BF16), "core", swap)
     chip_part = step_part[:lines] + piece.astype(F32)
-    piece = lax.ppermute(chip_part[lines // 2 :].astype(BF16), "hop", swap)
+    piece = lax.ppermute(chip_part[lines // 2 :].astype(BF16), "step", swap)
     hop_part = chip_part[: lines // 2] + piece.astype(F32)
     far = []
     for k in (1, 2):

time: 97.3 us -> 99.2 us (1.020)
  starting transfers between devices: 44.7 us -> 45.9 us
    ppermute x2, starting transfers between devices: 10.5 us -> 13 us  [body(): far.append(lax.ppermute(hop_part[k].astype(BF16), 'third', route))]
    all_to_all x1, starting transfers between devices: 12.5 us -> 11.1 us  [body(): lax.all_to_all(dq, members, split_axis=0, concat_axis=0, tiled=True)]
where the time goes in v7:
time: 99.2 us; the launch traced here: 97.5 us
  starting transfers between devices  45.9 us (46%)
  blocking collectives  27.5 us (28%)
  Pallas kernels  11.8 us (12%)
  waiting for transfers between devices  9.68 us (10%)
  local copies, waits for them, and re-layouts  1.03 us (1%)
    all_gather x1, blocking collectives, body(): kv_whole = lax.all_gather(kv_mine, REGION, axis=0, tiled=True)  27.5 us
    all_to_all x1, starting transfers between devices, body(): lax.all_to_all(sent, members, split_axis=0, concat_axis=0, tiled=True)  14.7 us
    ppermute x2, starting transfers between devices, body(): far.append(lax.ppermute(hop_part[k].astype(BF16), 'third', route))  13 us
    all_to_all x1, starting transfers between devices, body(): lax.all_to_all(dq, members, split_axis=0, concat_axis=0, tiled=True)  11.1 us
    pallas_call x1, Pallas kernels, attention_call(): pl.pallas_call(attention_kernel, out_shape=(jax.ShapeDtypeStruct((blocks,...  7.76 us
    ppermute x1, waiting for transfers between devices, body(): piece = lax.ppermute(chip_part[lines // 2:].astype(BF16), 'step', swap)  3.2 us
    pallas_call x1, Pallas kernels, pack_call(): pl.pallas_call(pack_kernel, grid=(PACK_STEPS,), out_shape=jax.ShapeDtypeS...  3.02 us
    ppermute x1, starting transfers between devices, body(): piece = lax.ppermute(given, 'hop', swap)  2.8 us
  transfers between devices with their start and end apart: 7, of which 4 were waited for; matrix products, arithmetic and copies ran while one was open for 1% of the time, Pallas kernels for 1%

profile of v7, /device:TPU:1, one launch (start us, length us, event | category | flops | bytes accessed | tf_op | source)
XLA Modules:
  0.0 97.5 jit_solution(7957117400579305241)
XLA Ops:
  0.6 0.0 copy-start
  0.6 3.0 %pack.1 = bf16[64,72,128]{2,1,0:T(8,128)(2,1)} custom-call(bf16[128,2048]{1,0:T(8,128)(2,1)} %q_ref.1, bf16[128,2048]{1,0:T(8,128)(2,1)} %g_ref.1, bf16[128,2048]{1,0:T(8,128)(2,1)} %o_ref.1), custom_call_target="tpu_custom_call" | custom-call | tf_op jit(solution)/shard_map/pack/pallas_call | solution.py:208
  3.7 0.0 copy-start.1
  3.7 0.0 copy-start.2
  3.7 14.7 %all-to-all-start = ((bf16[64,72,128]{2,1,0:T(8,128)(2,1)}), bf16[64,72,128]{2,1,0:T(8,128)(2,1)S(1)}, u32[]{:S(2)}, u32[]{:S(2)}) async-start(bf16[64,72,128]{2,1,0:T(8,128)(2,1)} %pack.1), calls=%async_computation | async-start | bytes 2359296 | tf_op jit(solution)/shard_map/all_to_all | solution.py:256
  18.4 0.1 pad_add_fusion.place_ref
  18.5 0.0 copy-done
  18.5 27.5 %all_gather.3 = bf16[1536,128]{1,0:T(8,128)(2,1)S(1)} all-gather(bf16[128,128]{1,0:T(8,128)(2,1)S(1)} %constant_dynamic-slice_fusion), channel_id=1, replica_groups=mesh['third'=3,'hop'=2,'step'=2,'chip'=32,'core'=2] {'third','hop','step'}, dimensions={0}, use_global_device_ids=true | all-gather | bytes 425984 | tf_op jit(solution)/shard_map/all_gather | solution.py:259
  46.1 1.0 constant_dynamic-slice_fusion.1
  47.0 2.8 %all-to-all-done.x_ref = bf16[64,72,128]{2,1,0:T(8,128)(2,1)S(1)} async-done(((bf16[64,72,128]{2,1,0:T(8,128)(2,1)}), bf16[64,72,128]{2,1,0:T(8,128)(2,1)S(1)}, u32[]{:S(2)}, u32[]{:S(2)}) %all-to-all-start) | async-done | bytes 1179680 | tf_op jit(solution)/shard_map/all_to_all | solution.py:256
  49.8 0.0 copy-done.1
  49.8 0.0 copy-done.2
  49.8 7.8 %attention.1 = (bf16[64,32,128]{2,1,0:T(8,128)(2,1)}, f32[12,64,128]{2,1,0:T(8,128)S(1)}, bf16[12,64,128]{2,1,0:T(8,128)(2,1)S(1)}) custom-call(s32[8,128]{1,0:T(8,128)S(1)} %bitcast.21, s32[128]{0:T(128)S(1)} %copy-done.2, s32[2]{0:T(128)S(1)} %pad_add_fusion.place_ref, bf16[64,72,128]{2,1,0:T(8,128)(2,1)S(1)} %all-to-all-done.x_ref, ...), custom_call_target="tpu_custom_call" | custom-call | tf_op jit(solution)/shard_map/attention/pallas_call | solution.py:225
  57.6 2.8 %collective-permute-start = (bf16[12,64,128]{2,1,0:T(8,128)(2,1)S(1)}, bf16[12,64,128]{2,1,0:T(8,128)(2,1)S(1)}, u32[]{:S(2)}, u32[]{:S(2)}) collective-permute-start(bf16[12,64,128]{2,1,0:T(8,128)(2,1)S(1)} %get-tuple-element.10), channel_id=1, source_target_pairs={{0,128},{128,0},{1,129},{129,1},{2,130},{130,2},{3,131},{131,3},{4... | collective-permute-start | bytes 589832 | tf_op jit(solution)/shard_map/ppermute | solution.py:272
  60.4 11.1 %all-to-all-start.1 = ((bf16[64,32,128]{2,1,0:T(8,128)(2,1)}), bf16[64,32,128]{2,1,0:T(8,128)(2,1)S(1)}, u32[]{:S(2)}, u32[]{:S(2)}) async-start(bf16[64,32,128]{2,1,0:T(8,128)(2,1)} %get-tuple-element.8), calls=%async_computation.1 | async-start | bytes 1048576 | tf_op jit(solution)/shard_map/all_to_all | solution.py:270
  71.4 0.0 collective-permute-done
  71.4 0.1 convert_add_fusion
  71.5 2.4 %collective-permute-start.1 = (bf16[6,64,128]{2,1,0:T(8,128)(2,1)S(1)}, bf16[6,64,128]{2,1,0:T(8,128)(2,1)S(1)}, u32[]{:S(2)}, u32[]{:S(2)}) collective-permute-start(bf16[6,64,128]{2,1,0:T(8,128)(2,1)S(1)} %slice.52), channel_id=1, source_target_pairs={{0,1},{1,0},{2,3},{3,2},{4,5},{5,4},{6,7},{7,6},{8,9},{9,8},{10,11... | collective-permute-start | bytes 294920 | tf_op jit(solution)/shard_map/ppermute | solution.py:275
  73.9 0.9 collective-permute-done.1
  74.9 1.9 %collective-permute-start.2 = (bf16[3,64,128]{2,1,0:T(8,128)(2,1)S(1)}, bf16[3,64,128]{2,1,0:T(8,128)(2,1)S(1)}, u32[]{:S(2)}, u32[]{:S(2)}) collective-permute-start(bf16[3,64,128]{2,1,0:T(8,128)(2,1)S(1)} %slice.53), channel_id=1, source_target_pairs={{0,64},{64,0},{1,65},{65,1},{2,66},{66,2},{3,67},{67,3},{4,68},{68... | collective-permute-start | bytes 147464 | tf_op jit(solution)/shard_map/ppermute | solution.py:277
  76.8 3.2 %collective-permute-done.2 = bf16[3,64,128]{2,1,0:T(8,128)(2,1)S(1)} collective-permute-done((bf16[3,64,128]{2,1,0:T(8,128)(2,1)S(1)}, bf16[3,64,128]{2,1,0:T(8,128)(2,1)S(1)}, u32[]{:S(2)}, u32[]{:S(2)}) %collective-permute-start.2) | collective-permute-done | bytes 49184 | tf_op jit(solution)/shard_map/ppermute | solution.py:277
  80.0 8.2 %collective-permute-start.3 = (bf16[64,128]{1,0:T(8,128)(2,1)S(1)}, bf16[64,128]{1,0:T(8,128)(2,1)S(1)}, u32[]{:S(2)}, u32[]{:S(2)}) collective-permute-start(bf16[64,128]{1,0:T(8,128)(2,1)S(1)} %get-tuple-element.17), channel_id=1, source_target_pairs={{0,256},{256,512},{512,0},{1,257},{257,513},{513,1},{2,258},{258,5... | collective-permute-start | bytes 49160 | tf_op jit(solution)/shard_map/ppermute | solution.py:282
  88.3 4.8 %collective-permute-start.4 = (bf16[64,128]{1,0:T(8,128)(2,1)S(1)}, bf16[64,128]{1,0:T(8,128)(2,1)S(1)}, u32[]{:S(2)}, u32[]{:S(2)}) collective-permute-start(bf16[64,128]{1,0:T(8,128)(2,1)S(1)} %get-tuple-element.16), channel_id=1, source_target_pairs={{0,512},{256,0},{512,256},{1,513},{257,1},{513,257},{2,514},{258,2... | collective-permute-start | bytes 49160 | tf_op jit(solution)/shard_map/ppermute | solution.py:282
  93.1 0.0 all-to-all-done.1.y_ref
  93.1 1.0 %unpack.1 = bf16[128,2048]{1,0:T(8,128)(2,1)} custom-call(bf16[64,32,128]{2,1,0:T(8,128)(2,1)S(1)} %all-to-all-done.1.y_ref), custom_call_target="tpu_custom_call" | custom-call | tf_op jit(solution)/shard_map/unpack/pallas_call | solution.py:283
  94.1 0.0 collective-permute-done.3
  94.1 2.8 %collective-permute-done.4 = bf16[64,128]{1,0:T(8,128)(2,1)S(1)} collective-permute-done((bf16[64,128]{1,0:T(8,128)(2,1)S(1)}, bf16[64,128]{1,0:T(8,128)(2,1)S(1)}, u32[]{:S(2)}, u32[]{:S(2)}) %collective-permute-start.4) | collective-permute-done | bytes 16416 | tf_op jit(solution)/shard_map/ppermute | solution.py:282
  96.9 0.6 fusion.2
  (6 shorter events, 0.1 us)
Async XLA Ops:
  0.6 17.9 %copy-start = (bf16[128,4096]{1,0:T(8,128)(2,1)S(1)}, bf16[128,4096]{1,0:T(8,128)(2,1)}, u32[]{:S(2)}) copy-start(bf16[128,4096]{1,0:T(8,128)(2,1)} %param.11) | copy-start | bytes 3145732
  3.7 46.1 %copy-start.1 = (s32[128,8]{0,1:T(8,128)S(1)}, s32[128,8]{0,1:T(8,128)}, u32[]{:S(2)}) copy-start(s32[128,8]{0,1:T(8,128)} %param.12) | copy-start | bytes 12292
  3.7 46.1 %copy-start.2 = (s32[128]{0:T(128)S(1)}, s32[128]{0:T(128)}, u32[]{:S(2)}) copy-start(s32[128]{0:T(128)} %counts_ref.1) | copy-start | bytes 1540
  3.7 46.1 %all-to-all-start = ((bf16[64,72,128]{2,1,0:T(8,128)(2,1)}), bf16[64,72,128]{2,1,0:T(8,128)(2,1)S(1)}, u32[]{:S(2)}, u32[]{:S(2)}) async-start(bf16[64,72,128]{2,1,0:T(8,128)(2,1)} %pack.1), calls=%async_computation | async-start | bytes 2359296 | tf_op jit(solution)/shard_map/all_to_all | solution.py:256
  57.6 13.9 %collective-permute-start = (bf16[12,64,128]{2,1,0:T(8,128)(2,1)S(1)}, bf16[12,64,128]{2,1,0:T(8,128)(2,1)S(1)}, u32[]{:S(2)}, u32[]{:S(2)}) collective-permute-start(bf16[12,64,128]{2,1,0:T(8,128)(2,1)S(1)} %get-tuple-element.10), channel_id=1, source_target_pairs={{0,128},{128,0},{1,129},{129,1},{2,130},{130,2},{3,131},{131,3},{4... | collective-permute-start | bytes 589832 | tf_op jit(solution)/shard_map/ppermute | solution.py:272
  60.4 32.7 %all-to-all-start.1 = ((bf16[64,32,128]{2,1,0:T(8,128)(2,1)}), bf16[64,32,128]{2,1,0:T(8,128)(2,1)S(1)}, u32[]{:S(2)}, u32[]{:S(2)}) async-start(bf16[64,32,128]{2,1,0:T(8,128)(2,1)} %get-tuple-element.8), calls=%async_computation.1 | async-start | bytes 1048576 | tf_op jit(solution)/shard_map/all_to_all | solution.py:270
  71.5 3.3 %collective-permute-start.1 = (bf16[6,64,128]{2,1,0:T(8,128)(2,1)S(1)}, bf16[6,64,128]{2,1,0:T(8,128)(2,1)S(1)}, u32[]{:S(2)}, u32[]{:S(2)}) collective-permute-start(bf16[6,64,128]{2,1,0:T(8,128)(2,1)S(1)} %slice.52), channel_id=1, source_target_pairs={{0,1},{1,0},{2,3},{3,2},{4,5},{5,4},{6,7},{7,6},{8,9},{9,8},{10,11... | collective-permute-start | bytes 294920 | tf_op jit(solution)/shard_map/ppermute | solution.py:275
  74.9 5.1 %collective-permute-start.2 = (bf16[3,64,128]{2,1,0:T(8,128)(2,1)S(1)}, bf16[3,64,128]{2,1,0:T(8,128)(2,1)S(1)}, u32[]{:S(2)}, u32[]{:S(2)}) collective-permute-start(bf16[3,64,128]{2,1,0:T(8,128)(2,1)S(1)} %slice.53), channel_id=1, source_target_pairs={{0,64},{64,0},{1,65},{65,1},{2,66},{66,2},{3,67},{67,3},{4,68},{68... | collective-permute-start | bytes 147464 | tf_op jit(solution)/shard_map/ppermute | solution.py:277
  80.0 14.1 %collective-permute-start.3 = (bf16[64,128]{1,0:T(8,128)(2,1)S(1)}, bf16[64,128]{1,0:T(8,128)(2,1)S(1)}, u32[]{:S(2)}, u32[]{:S(2)}) collective-permute-start(bf16[64,128]{1,0:T(8,128)(2,1)S(1)} %get-tuple-element.17), channel_id=1, source_target_pairs={{0,256},{256,512},{512,0},{1,257},{257,513},{513,1},{2,258},{258,5... | collective-permute-start | bytes 49160 | tf_op jit(solution)/shard_map/ppermute | solution.py:282
  88.3 8.7 %collective-permute-start.4 = (bf16[64,128]{1,0:T(8,128)(2,1)S(1)}, bf16[64,128]{1,0:T(8,128)(2,1)S(1)}, u32[]{:S(2)}, u32[]{:S(2)}) collective-permute-start(bf16[64,128]{1,0:T(8,128)(2,1)S(1)} %get-tuple-element.16), channel_id=1, source_target_pairs={{0,512},{256,0},{512,256},{1,513},{257,1},{513,257},{2,514},{258,2... | collective-permute-start | bytes 49160 | tf_op jit(solution)/shard_map/ppermute | solution.py:282
